TPU v7x, 512 devices: a whole 4x8x8 slice. The times are simulated.
512 devices in a mesh: layer: 32 (over z, y_hi, core), prow: 4 (over x), pcol: 4 (over y_lo).
Axes of the slice: x: 4, y: 8 (y_hi: 2, y_lo: 4; y = y_hi * 4 + y_lo), z: 8, core: 2. Of those that a mesh axis runs over, the one named last changes fastest.
Arguments:
- subtree_right_hand: bfloat16 [32, 6144, 512], P('layer', ('prow', 'pcol')), may hold values from -6 to 6
- root_rhs: bfloat16 [2048, 512], P(('prow', 'pcol')), may hold values from -6 to 6
- blocks: bfloat16 [32, 6, 4, 4, 4, 4, 128, 128], P('layer', None, 'prow', 'pcol'), may hold values from -0.1875 to 0.1875
- pattern: int32 [32, 6, 4, 4, 4, 4], P('layer', None, 'prow', 'pcol'), may hold values 0 or 1
- forest_inverse: float32 [32, 3, 4, 4, 128, 128], P('layer', None, 'prow', 'pcol'), may hold values from -0.5 to 0.5
- root_inverse: float32 [4, 4, 128, 128], P('prow', 'pcol'), may hold values from -0.5 to 0.5
Outputs:
- forest_solution: bfloat16 [32, 6144, 512], P('layer', ('prow', 'pcol'))
- root_solution: bfloat16 [2048, 512], P(('prow', 'pcol'))
All inputs are finite; a program needn't handle non-finite values. No bound on the sum of `pattern` on one device may be relied on, other than what follows from the above.
Results may differ from a plain program's by a relative error of at most 0.0057.
Values may be sent and summed in bfloat16 or wider, within the bound.
A program may use at most 64 MiB of HBM per device.

v0:
```python
import jax
import jax.numpy as jnp
from jax import lax
from jax.sharding import PartitionSpec as P


def pair_slot(source, target):
    return (0, 3, 5)[source] + target - source - 1


def shards(subtree_right_hand, root_rhs, blocks, pattern, forest_inverse, root_inverse):
    grid_size = lax.axis_size("prow")
    super_rows = blocks.shape[-1]
    rhs_cols = subtree_right_hand.shape[-1]
    slice_rows = super_rows // grid_size
    local_forest = subtree_right_hand.reshape(3, grid_size, slice_rows, rhs_cols)
    local_root = root_rhs.reshape(1, grid_size, slice_rows, rhs_cols)
    joined = jnp.concatenate([local_forest, local_root], axis=0)
    placed = lax.all_to_all(
        lax.all_to_all(joined, "prow", split_axis=1, concat_axis=1, tiled=True),
        "pcol",
        split_axis=1,
        concat_axis=1,
        tiled=True,
    )
    placed = placed.reshape(4, super_rows, rhs_cols)
    block_mask = pattern.reshape(6, grid_size, grid_size).astype(jnp.bfloat16)
    masked = (
        blocks.reshape(6, grid_size, grid_size, super_rows, super_rows)
        * block_mask[..., None, None]
    )
    inverses = forest_inverse.reshape(3, super_rows, super_rows)
    solved = []
    empty_rows = jnp.zeros((grid_size, super_rows, rhs_cols), jnp.float32)
    totals = (empty_rows, empty_rows, empty_rows, empty_rows)
    for tier_index in range(3):
        right_hand_side = placed[tier_index].astype(jnp.float32)
        if tier_index > 0:
            reduced = lax.psum_scatter(totals[tier_index], "pcol", scatter_dimension=0, tiled=True)
            right_hand_side = right_hand_side - reduced[0]
        answer = jnp.dot(
            inverses[tier_index],
            right_hand_side,
            precision=lax.Precision.HIGHEST,
            preferred_element_type=jnp.float32,
        ).astype(jnp.bfloat16)
        solved.append(answer)

        def update(running, block_pieces, first_row, tier_index=tier_index):
            count = block_pieces.shape[0]
            updated_rows = []
            for target in range(4):
                if target > tier_index:
                    factor_weights = masked[pair_slot(tier_index, target)]
                    term = jnp.einsum(
                        "jznv,zvs->jns",
                        factor_weights,
                        block_pieces,
                        preferred_element_type=jnp.float32,
                    )
                    updated_rows.append(running[target] + term)
                else:
                    updated_rows.append(running[target])
            return tuple(updated_rows)

        totals = update(
            totals, lax.all_gather(answer[None], "prow", axis=0, tiled=True), jnp.int32(0)
        )
    row_share = lax.psum_scatter(totals[3], "pcol", scatter_dimension=0, tiled=True)
    reduced_root = lax.psum(row_share[0], "layer")
    root_side = placed[3].astype(jnp.float32) - reduced_root
    root_answer = jnp.dot(
        root_inverse.reshape(super_rows, super_rows),
        root_side,
        precision=lax.Precision.HIGHEST,
        preferred_element_type=jnp.float32,
    ).astype(jnp.bfloat16)
    stacked = jnp.stack(solved + [root_answer]).reshape(4, grid_size, slice_rows, rhs_cols)
    returned = lax.all_to_all(
        lax.all_to_all(stacked, "pcol", split_axis=1, concat_axis=1, tiled=True),
        "prow",
        split_axis=1,
        concat_axis=1,
        tiled=True,
    )
    forest_out = returned[:3].reshape(1, 3 * super_rows, rhs_cols)
    root_out = returned[3].reshape(super_rows, rhs_cols)
    return (forest_out, root_out)


def solution(mesh):
    placed = (
        P("layer", ("prow", "pcol"), None),
        P(("prow", "pcol"), None),
        P("layer", None, "prow", "pcol", None, None, None, None),
        P("layer", None, "prow", "pcol", None, None),
        P("layer", None, "prow", "pcol", None, None),
        P("prow", "pcol", None, None),
    )
    return jax.shard_map(
        shards,
        mesh=mesh,
        in_specs=placed,
        out_specs=(P("layer", ("prow", "pcol"), None), P(("prow", "pcol"), None)),
        check_vma=False,
    )
```

profile of v0, /device:TPU:6, one launch (start us, length us, event | category | flops | bytes accessed | tf_op | source)
XLA Modules:
  0.0 581.1 jit_solution(10814355809280469944)
XLA Ops:
  7.2 0.0 copy-start
  7.2 0.0 copy-start.7
  7.2 1.1 pad_maximum_fusion
  8.4 14.9 %all_to_all.20 = bf16[4,4,32,512]{3,2,0,1:T(8,128)(2,1)} all-to-all(bf16[4,4,32,512]{3,2,0,1:T(8,128)(2,1)S(1)} %copy.14), channel_id=1, replica_groups=mesh['layer'=32,'prow'=4,'pcol'=4] {'prow'}, dimensions={1} | all-to-all | bytes 1048576 | tf_op jit(solution)/shard_map/all_to_all | solution.py:20
  23.3 4.1 all-to-all-start.1
  27.5 0.0 reduce-scatter.4.cloned.1.call-start
  27.5 0.0 copy-done.7
  27.5 0.1 copy.15
  27.7 2.2 bitcast_multiply_fusion
  29.8 8.9 %all-to-all-done.1 = bf16[4,4,32,512]{3,2,0,1:T(8,128)(2,1)} async-done(((bf16[4,4,32,512]{3,2,0,1:T(8,128)(2,1)}), bf16[4,4,32,512]{3,2,0,1:T(8,128)(2,1)}, u32[]{:S(2)}, u32[]{:S(2)}) %all-to-all-start.1) | async-done | bytes 524320 | tf_op jit(solution)/shard_map/all_to_all | solution.py:19
  38.7 1.8 fusion.14
  40.6 1.1 convolution_convert_fusion.3
  41.7 13.3 %all-gather = bf16[512,512]{1,0:T(8,128)(2,1)S(1)} all-gather(bf16[128,512]{1,0:T(8,128)(2,1)S(1)} %bitcast.118), channel_id=2, replica_groups=mesh['layer'=32,'prow'=4,'pcol'=4] {'prow'}, dimensions={0}, use_global_device_ids=true | all-gather | bytes 655360 | tf_op jit(solution)/shard_map/all_gather | solution.py:67
  55.0 0.0 copy-start.1
  55.0 0.8 copy-done.1
  55.8 1.4 convolution_bitcast_fusion.5
  57.2 0.0 reduce-scatter.4.cloned.1.call-update
  57.3 0.0 reduce-scatter.6.cloned.1.call-start
  57.3 39.3 %reduce-scatter.4.cloned.1.call-done = f32[1,128,512]{2,1,0:T(8,128)} async-done(((f32[4,128,512]{2,1,0:T(8,128)}), f32[1,128,512]{2,1,0:T(8,128)}) %reduce-scatter.4.cloned.1.call-update) | async-done | bytes 262160 | tf_op jit(solution)/shard_map/reduce_scatter | solution.py:39
  96.6 0.0 copy-start.2
  96.6 1.5 convolution_convert_fusion.2
  98.1 13.4 %all-gather.1 = bf16[512,512]{1,0:T(8,128)(2,1)S(1)} all-gather(bf16[128,512]{1,0:T(8,128)(2,1)S(1)} %bitcast.120), channel_id=3, replica_groups=mesh['layer'=32,'prow'=4,'pcol'=4] {'prow'}, dimensions={0}, use_global_device_ids=true | all-gather | bytes 655360 | tf_op jit(solution)/shard_map/all_gather | solution.py:67
  111.5 0.0 copy-start.4
  111.5 0.8 copy-done.4
  112.3 0.4 convolution_bitcast_fusion.3
  112.7 0.0 copy-done.2
  112.7 1.4 fusion
  114.2 0.0 reduce-scatter.6.cloned.1.call-update
  114.2 0.0 reduce-scatter.8.cloned.1.call-start
  114.2 2.4 convolution_bitcast_fusion.1
  116.7 31.5 %reduce-scatter.6.cloned.1.call-done = f32[1,128,512]{2,1,0:T(8,128)} async-done(((f32[4,128,512]{2,1,0:T(8,128)}), f32[1,128,512]{2,1,0:T(8,128)}) %reduce-scatter.6.cloned.1.call-update) | async-done | bytes 262160 | tf_op jit(solution)/shard_map/reduce_scatter | solution.py:39
  148.2 0.0 copy-start.3
  148.2 0.0 copy-start.5
  148.2 1.5 convolution_convert_fusion.1
  149.8 0.0 copy-start.6
  149.8 13.4 %all-gather.2 = bf16[512,512]{1,0:T(8,128)(2,1)S(1)} all-gather(bf16[128,512]{1,0:T(8,128)(2,1)S(1)} %bitcast.122), channel_id=4, replica_groups=mesh['layer'=32,'prow'=4,'pcol'=4] {'prow'}, dimensions={0}, use_global_device_ids=true | all-gather | bytes 655360 | tf_op jit(solution)/shard_map/all_gather | solution.py:67
  163.2 0.0 copy-done.6
  163.2 0.4 convolution_bitcast_fusion
  163.6 0.0 copy-done.3
  163.6 0.0 copy-done.5
  163.6 1.4 fusion.2
  165.0 0.0 reduce-scatter.8.cloned.1.call-update
  165.1 0.0 all-reduce.2.cloned.1.call-start
  165.1 33.9 %reduce-scatter.8.cloned.1.call-done = f32[1,128,512]{2,1,0:T(8,128)} async-done(((f32[4,128,512]{2,1,0:T(8,128)}), f32[1,128,512]{2,1,0:T(8,128)}) %reduce-scatter.8.cloned.1.call-update) | async-done | bytes 262160 | tf_op jit(solution)/shard_map/reduce_scatter | solution.py:69
  199.0 0.0 all-reduce.2.cloned.1.call-update
  199.0 343.4 %all-reduce.2.cloned.1.call-done = f32[128,512]{1,0:T(8,128)} async-done(((f32[128,512]{1,0:T(8,128)}), f32[128,512]{1,0:T(8,128)}) %all-reduce.2.cloned.1.call-update) | async-done | bytes 262160 | tf_op jit(solution)/shard_map/psum | solution.py:70
  542.4 0.0 copy-done
  542.4 1.4 convolution_convert_fusion
  543.8 1.0 pad_maximum_fusion.1
  544.8 17.5 %all_to_all.21 = bf16[4,4,32,512]{3,2,0,1:T(8,128)(2,1)S(1)} all-to-all(bf16[4,4,32,512]{3,2,0,1:T(8,128)(2,1)S(1)} %pad_maximum_fusion.1), channel_id=1, replica_groups=mesh['layer'=32,'prow'=4,'pcol'=4] {'pcol'}, dimensions={1} | all-to-all | bytes 1048576 | tf_op jit(solution)/shard_map/all_to_all | solution.py:80
  562.3 10.8 %all_to_all.22 = bf16[4,4,32,512]{3,2,0,1:T(8,128)(2,1)S(1)} all-to-all(bf16[4,4,32,512]{3,2,0,1:T(8,128)(2,1)S(1)} %all_to_all.21), channel_id=1, replica_groups=mesh['layer'=32,'prow'=4,'pcol'=4] {'prow'}, dimensions={1} | all-to-all | bytes 1048576 | tf_op jit(solution)/shard_map/all_to_all | solution.py:79
  573.1 0.8 copy.27
  573.9 0.7 slice.78
  (3 shorter events, 0.1 us)
Async XLA Ops:
  7.2 535.2 %copy-start = (f32[1,1,128,128]{3,2,1,0:T(8,128)S(1)}, f32[1,1,128,128]{3,2,1,0:T(8,128)}, u32[]{:S(2)}) copy-start(f32[1,1,128,128]{3,2,1,0:T(8,128)} %param.11) | copy-start | bytes 196612
  7.2 20.3 %copy-start.7 = (s32[1,6,1,1,4,4]{1,5,4,3,2,0:T(4,128)S(1)}, s32[1,6,1,1,4,4]{1,5,4,3,2,0:T(4,128)}, u32[]{:S(2)}) copy-start(s32[1,6,1,1,4,4]{1,5,4,3,2,0:T(4,128)} %param.9) | copy-start | bytes 1156
  23.3 15.4 %all-to-all-start.1 = ((bf16[4,4,32,512]{3,2,0,1:T(8,128)(2,1)}), bf16[4,4,32,512]{3,2,0,1:T(8,128)(2,1)}, u32[]{:S(2)}, u32[]{:S(2)}) async-start(bf16[4,4,32,512]{3,2,0,1:T(8,128)(2,1)} %all_to_all.20), calls=%async_computation.1 | async-start | bytes 1048576 | tf_op jit(solution)/shard_map/all_to_all | solution.py:19
  27.5 69.1 %reduce-scatter.4.cloned.1.call-start = ((), (), s32[]{:S(2)}) async-start(), calls=%async_computation.7 | async-start | bytes 1310720 | tf_op jit(solution)/shard_map/reduce_scatter | solution.py:39
  55.0 0.8 copy-start.1
  57.3 90.9 %reduce-scatter.6.cloned.1.call-start = ((), (), s32[]{:S(2)}) async-start(), calls=%async_computation.8 | async-start | bytes 1310720 | tf_op jit(solution)/shard_map/reduce_scatter | solution.py:39
  96.6 16.1 %copy-start.2 = (bf16[512,512]{1,0:T(8,128)(2,1)S(1)}, bf16[512,512]{1,0:T(8,128)(2,1)}, u32[]{:S(2)}) copy-start(bf16[512,512]{1,0:T(8,128)(2,1)} %copy-done.1) | copy-start | bytes 1572868
  111.5 0.8 copy-start.4
  114.2 84.8 %reduce-scatter.8.cloned.1.call-start = ((), (), s32[]{:S(2)}) async-start(), calls=%async_computation.9 | async-start | bytes 1310720 | tf_op jit(solution)/shard_map/reduce_scatter | solution.py:69
  148.2 15.4 %copy-start.3 = (bf16[512,512]{1,0:T(8,128)(2,1)S(1)}, bf16[512,512]{1,0:T(8,128)(2,1)}, u32[]{:S(2)}) copy-start(bf16[512,512]{1,0:T(8,128)(2,1)} %copy-done.1) | copy-start | bytes 1572868
  148.2 15.4 %copy-start.5 = (f32[4,128,512]{2,1,0:T(8,128)S(1)}, f32[4,128,512]{2,1,0:T(8,128)}, u32[]{:S(2)}) copy-start(f32[4,128,512]{2,1,0:T(8,128)} %convolution_bitcast_fusion.1) | copy-start | bytes 3145732
  149.8 13.4 %copy-start.6 = (bf16[512,128]{0,1:T(8,128)(2,1)}, bf16[512,128]{0,1:T(8,128)(2,1)S(1)}, u32[]{:S(2)}) copy-start(bf16[512,128]{0,1:T(8,128)(2,1)S(1)} %convolution_convert_fusion.1) | copy-start | bytes 393220
  165.1 377.4 %all-reduce.2.cloned.1.call-start = ((), (), s32[]{:S(2)}) async-start(), calls=%async_computation.10 | async-start | bytes 524288 | tf_op jit(solution)/shard_map/psum | solution.py:70
Sparse Core Ops, SparseCore 0:
  57.4 39.1 reduce-scatter.3
  114.3 33.8 reduce-scatter.5
  165.2 33.7 reduce-scatter.7
  202.0 340.3 all-reduce.1
where the time goes:
time: 582 us; the launch traced here: 581 us
  waiting for transfers between devices  457 us (79%)
  blocking collectives  83.3 us (14%)
  between operations  13.9 us (2%)
  matrix products  13.1 us (2%)
    psum x1, waiting for transfers between devices, shards(): reduced_root = lax.psum(row_share[0], 'layer')  343 us
    reduce_scatter x2, waiting for transfers between devices, shards(): lax.psum_scatter(totals[tier_index], 'pcol', scatter_dimension=0, tiled=T...  70.8 us
    all_gather x3, blocking collectives, shards(): lax.all_gather(answer[None], 'prow', axis=0, tiled=True)  40.1 us
    reduce_scatter x1, waiting for transfers between devices, shards(): lax.psum_scatter(totals[3], 'pcol', scatter_dimension=0, tiled=True)  33.9 us
    all_to_all x1, blocking collectives, shards(): lax.all_to_all(stacked, 'pcol', split_axis=1, concat_axis=1, tiled=True)  17.5 us
    all_to_all x1, blocking collectives, shards(): lax.all_to_all(joined, 'prow', split_axis=1, concat_axis=1, tiled=True)  14.9 us
  transfers between devices with their start and end apart: 5, of which 5 were waited for; matrix products, arithmetic and copies ran while one was open for 1% of the time, Pallas kernels for 0%

commit v1 on v0

--- a/solution.py
+++ b/solution.py
@@ -1,15 +1,145 @@
 import jax
 import jax.numpy as jnp
 from jax import lax
+from jax.experimental import pallas as pl
+from jax.experimental.pallas import tpu as pltpu
 from jax.sharding import PartitionSpec as P
+
+MESH = pl.DeviceIdType.MESH
+VMEM_SPEC = pl.BlockSpec(memory_space=pltpu.VMEM)
 
 
 def pair_slot(source, target):
     return (0, 3, 5)[source] + target - source - 1
 
 
+def _barrier(axis, n, me):
+    barrier = pltpu.get_barrier_semaphore()
+    for d in range(1, n):
+        pl.semaphore_signal(barrier, 1, device_id={axis: (me + d) % n}, device_id_type=MESH)
+    pl.semaphore_wait(barrier, n - 1)
+
+
+def _params(cid):
+    return pltpu.CompilerParams(collective_id=cid, has_side_effects=True)
+
+
+def reduce_scatter(x, axis, cid):
+    n = x.shape[0]
+
+    def kernel(x_ref, o_ref, recv, ssem, rsem):
+        me = lax.axis_index(axis)
+        _barrier(axis, n, me)
+        copies = []
+        for d in range(1, n):
+            peer = (me + d) % n
+            copy = pltpu.make_async_remote_copy(
+                x_ref.at[peer], recv.at[d - 1], ssem.at[d - 1], rsem.at[d - 1],
+                device_id={axis: peer}, device_id_type=MESH)
+            copy.start()
+            copies.append(copy)
+        for copy in copies:
+            copy.wait()
+        total = x_ref[me]
+        for d in range(n - 1):
+            total = total + recv[d]
+        o_ref[...] = total
+
+    return pl.pallas_call(
+        kernel,
+        out_shape=jax.ShapeDtypeStruct(x.shape[1:], x.dtype),
+        in_specs=[VMEM_SPEC],
+        out_specs=VMEM_SPEC,
+        scratch_shapes=[
+            pltpu.VMEM((n - 1,) + x.shape[1:], x.dtype),
+            pltpu.SemaphoreType.DMA((n - 1,)),
+            pltpu.SemaphoreType.DMA((n - 1,)),
+        ],
+        compiler_params=_params(cid),
+    )(x)
+
+
+def all_gather(x, axis, n, cid):
+    def kernel(x_ref, o_ref, ssem, rsem):
+        me = lax.axis_index(axis)
+        _barrier(axis, n, me)
+        copies = []
+        for d in range(1, n):
+            peer = (me + d) % n
+            copy = pltpu.make_async_remote_copy(
+                x_ref, o_ref.at[me], ssem.at[d - 1], rsem.at[d - 1],
+                device_id={axis: peer}, device_id_type=MESH)
+            copy.start()
+            copies.append(copy)
+        o_ref[me] = x_ref[...]
+        for copy in copies:
+            copy.wait()
+
+    return pl.pallas_call(
+        kernel,
+        out_shape=jax.ShapeDtypeStruct((n,) + x.shape, x.dtype),
+        in_specs=[VMEM_SPEC],
+        out_specs=VMEM_SPEC,
+        scratch_shapes=[
+            pltpu.SemaphoreType.DMA((n - 1,)),
+            pltpu.SemaphoreType.DMA((n - 1,)),
+        ],
+        compiler_params=_params(cid),
+    )(x)
+
+
+def all_reduce(x, axis, cid):
+    n = x.shape[0]
+
+    def kernel(x_ref, o_ref, recv, part, ssem, rsem, gsem, hsem):
+        me = lax.axis_index(axis)
+        _barrier(axis, n, me)
+        copies = []
+        for d in range(1, n):
+            peer = (me + d) % n
+            copy = pltpu.make_async_remote_copy(
+                x_ref.at[peer], recv.at[d - 1], ssem.at[d - 1], rsem.at[d - 1],
+                device_id={axis: peer}, device_id_type=MESH)
+            copy.start()
+            copies.append(copy)
+        for copy in copies:
+            copy.wait()
+        total = x_ref[me]
+        for d in range(n - 1):
+            total = total + recv[d]
+        part[...] = total
+        o_ref[me] = total
+        copies = []
+        for d in range(1, n):
+            peer = (me + d) % n
+            copy = pltpu.make_async_remote_copy(
+                part, o_ref.at[me], gsem.at[d - 1], hsem.at[d - 1],
+                device_id={axis: peer}, device_id_type=MESH)
+            copy.start()
+            copies.append(copy)
+        for copy in copies:
+            copy.wait()
+
+    return pl.pallas_call(
+        kernel,
+        out_shape=jax.ShapeDtypeStruct(x.shape, x.dtype),
+        in_specs=[VMEM_SPEC],
+        out_specs=VMEM_SPEC,
+        scratch_shapes=[
+            pltpu.VMEM((n - 1,) + x.shape[1:], x.dtype),
+            pltpu.VMEM(x.shape[1:], x.dtype),
+            pltpu.SemaphoreType.DMA((n - 1,)),
+            pltpu.SemaphoreType.DMA((n - 1,)),
+            pltpu.SemaphoreType.DMA((n - 1,)),
+            pltpu.SemaphoreType.DMA((n - 1,)),
+        ],
+        compiler_params=_params(cid),
+    )(x)
+
+
 def shards(subtree_right_hand, root_rhs, blocks, pattern, forest_inverse, root_inverse):
     grid_size = lax.axis_size("prow")
+    n_layer = lax.axis_size("layer")
     super_rows = blocks.shape[-1]
     rhs_cols = subtree_right_hand.shape[-1]
     slice_rows = super_rows // grid_size
@@ -36,8 +166,8 @@
     for tier_index in range(3):
         right_hand_side = placed[tier_index].astype(jnp.float32)
         if tier_index > 0:
-            reduced = lax.psum_scatter(totals[tier_index], "pcol", scatter_dimension=0, tiled=True)
-            right_hand_side = right_hand_side - reduced[0]
+            reduced = reduce_scatter(totals[tier_index], "pcol", 10 + tier_index)
+            right_hand_side = right_hand_side - reduced
         answer = jnp.dot(
             inverses[tier_index],
             right_hand_side,
@@ -45,29 +175,24 @@
             preferred_element_type=jnp.float32,
         ).astype(jnp.bfloat16)
         solved.append(answer)
-
-        def update(running, block_pieces, first_row, tier_index=tier_index):
-            count = block_pieces.shape[0]
-            updated_rows = []
-            for target in range(4):
-                if target > tier_index:
-                    factor_weights = masked[pair_slot(tier_index, target)]
-                    term = jnp.einsum(
-                        "jznv,zvs->jns",
-                        factor_weights,
-                        block_pieces,
-                        preferred_element_type=jnp.float32,
-                    )
-                    updated_rows.append(running[target] + term)
-                else:
-                    updated_rows.append(running[target])
-            return tuple(updated_rows)
-
-        totals = update(
-            totals, lax.all_gather(answer[None], "prow", axis=0, tiled=True), jnp.int32(0)
-        )
-    row_share = lax.psum_scatter(totals[3], "pcol", scatter_dimension=0, tiled=True)
-    reduced_root = lax.psum(row_share[0], "layer")
+        block_pieces = all_gather(answer, "prow", grid_size, 20 + tier_index)
+        updated_rows = []
+        for target in range(4):
+            if target > tier_index:
+                factor_weights = masked[pair_slot(tier_index, target)]
+                term = jnp.einsum(
+                    "jznv,zvs->jns",
+                    factor_weights,
+                    block_pieces,
+                    preferred_element_type=jnp.float32,
+                )
+                updated_rows.append(totals[target] + term)
+            else:
+                updated_rows.append(totals[target])
+        totals = tuple(updated_rows)
+    row_share = reduce_scatter(totals[3], "pcol", 13)
+    chunks = row_share.reshape(n_layer, -1, 128)
+    reduced_root = all_reduce(chunks, "layer", 30).reshape(super_rows, rhs_cols)
     root_side = placed[3].astype(jnp.float32) - reduced_root
     root_answer = jnp.dot(
         root_inverse.reshape(super_rows, super_rows),

time: 582 us -> 244 us (0.42)
  waiting for transfers between devices: 457 us -> 8.95 us
  Pallas kernels: 0 us -> 147 us
  blocking collectives: 83.3 us -> 49.8 us
  between operations: 13.9 us -> 0.84 us
  matrix products: 13.1 us -> 20.8 us
    psum x1 -> x0, waiting for transfers between devices: 343 us -> none  [shards(): reduced_root = lax.psum(row_share[0], 'layer')]
    pallas_call x0 -> x7, Pallas kernels: none -> 147 us  [the longest x3 76.3 us: reduce_scatter(): pl.pallas_call(kernel, out_shape=jax.ShapeDtypeStruct(x.shape[1:], x.dtyp...]
    reduce_scatter x3 -> x0, waiting for transfers between devices: 105 us -> none  [the longest x2 70.8 us: shards(): lax.psum_scatter(totals[tier_index], 'pcol', scatter_dimension=0, tiled=T...]
    all_gather x3 -> x0, blocking collectives: 40.1 us -> none  [shards(): lax.all_gather(answer[None], 'prow', axis=0, tiled=True)]
    dot_general x6, matrix products: 7.59 us -> 14.6 us  [shards(): jnp.einsum('jznv,zvs->jns', factor_weights, block_pieces, preferred_eleme...]
    all_to_all x1, blocking collectives: 17.5 us -> 23.9 us  [shards(): lax.all_to_all(stacked, 'pcol', split_axis=1, concat_axis=1, tiled=True)]
  transfers between devices with their start and end apart: 5 -> 1, of which waited for: 5 -> 1; matrix products, arithmetic and copies ran while one was open for 1% -> 1% of each run, Pallas kernels for 0% -> 0%
where the time goes in v1:
time: 244 us; the launch traced here: 242 us
  Pallas kernels  147 us (60%)
  blocking collectives  49.8 us (20%)
  matrix products  20.8 us (9%)
  waiting for transfers between devices  8.95 us (4%)
  other arithmetic  6.29 us (3%)
  starting transfers between devices  4.14 us (2%)
  local copies, waits for them, and re-layouts  4.08 us (2%)
    pallas_call x3, Pallas kernels, reduce_scatter(): pl.pallas_call(kernel, out_shape=jax.ShapeDtypeStruct(x.shape[1:], x.dtyp...  76.3 us
    pallas_call x1, Pallas kernels, all_reduce(): pl.pallas_call(kernel, out_shape=jax.ShapeDtypeStruct(x.shape, x.dtype),...  38.5 us
    pallas_call x3, Pallas kernels, all_gather(): pl.pallas_call(kernel, out_shape=jax.ShapeDtypeStruct((n,) + x.shape, x.d...  32.4 us
    all_to_all x1, blocking collectives, shards(): lax.all_to_all(stacked, 'pcol', split_axis=1, concat_axis=1, tiled=True)  23.9 us
    all_to_all x1, blocking collectives, shards(): lax.all_to_all(joined, 'prow', split_axis=1, concat_axis=1, tiled=True)  15 us
    dot_general x6, matrix products, shards(): jnp.einsum('jznv,zvs->jns', factor_weights, block_pieces, preferred_eleme...  14.6 us
    all_to_all x1, blocking collectives, shards(): lax.all_to_all(lax.all_to_all(stacked, 'pcol', split_axis=1, concat_axis=...  10.9 us
    all_to_all x1, waiting for transfers between devices, shards(): lax.all_to_all(lax.all_to_all(joined, 'prow', split_axis=1, concat_axis=1...  8.95 us
  transfers between devices with their start and end apart: 1, of which 1 were waited for; matrix products, arithmetic and copies ran while one was open for 1% of the time, Pallas kernels for 0%

profile of v1, /device:TPU:6, one launch (start us, length us, event | category | flops | bytes accessed | tf_op | source)
XLA Modules:
  0.0 242.0 jit_solution(5989276775450781655)
XLA Ops:
  0.6 0.0 copy-start
  0.6 0.0 copy-start.5
  0.7 1.1 pad_maximum_fusion
  1.9 15.0 %all_to_all.20 = bf16[4,4,32,512]{3,2,0,1:T(8,128)(2,1)} all-to-all(bf16[4,4,32,512]{3,2,0,1:T(8,128)(2,1)S(1)} %copy.14), channel_id=1, replica_groups=mesh['layer'=32,'prow'=4,'pcol'=4] {'prow'}, dimensions={1} | all-to-all | bytes 1048576 | tf_op jit(solution)/shard_map/all_to_all | solution.py:150
  16.8 4.1 %all-to-all-start.1 = ((bf16[4,4,32,512]{3,2,0,1:T(8,128)(2,1)}), bf16[4,4,32,512]{3,2,0,1:T(8,128)(2,1)}, u32[]{:S(2)}, u32[]{:S(2)}) async-start(bf16[4,4,32,512]{3,2,0,1:T(8,128)(2,1)} %all_to_all.20), calls=%async_computation.1 | async-start | bytes 1048576 | tf_op jit(solution)/shard_map/all_to_all | solution.py:149
  21.0 0.0 copy-done.5
  21.0 0.1 copy.15
  21.1 2.2 bitcast_multiply_fusion
  23.3 8.9 %all-to-all-done.1 = bf16[4,4,32,512]{3,2,0,1:T(8,128)(2,1)} async-done(((bf16[4,4,32,512]{3,2,0,1:T(8,128)(2,1)}), bf16[4,4,32,512]{3,2,0,1:T(8,128)(2,1)}, u32[]{:S(2)}, u32[]{:S(2)}) %all-to-all-start.1) | async-done | bytes 524320 | tf_op jit(solution)/shard_map/all_to_all | solution.py:149
  32.2 1.8 fusion.16
  34.1 1.7 convolution_convert_fusion.3
  35.8 10.0 %shard_map.77 = bf16[4,128,512]{2,1,0:T(8,128)(2,1)} custom-call(bf16[128,512]{1,0:T(8,128)(2,1)} %bitcast.108), custom_call_target="tpu_custom_call" | custom-call | tf_op jit(solution)/shard_map/pallas_call | solution.py:78
  45.9 2.4 %convolution_bitcast_fusion.5.x_ref = f32[4,128,512]{2,1,0:T(8,128)} fusion(bf16[6,4,4,128,128]{4,3,2,1,0:T(8,128)(2,1)S(1)} %bitcast_multiply_fusion, bf16[4,128,512]{2,1,0:T(8,128)(2,1)} %shard_map.77), kind=kOutput, calls=%fused_computation.6 | convolution fusion | flops 268435456 | bytes 2097152 | tf_op jit(solution)/shard_map/jznv,zvs->jns/dot_general | solution.py:183
  48.3 18.9 %shard_map.78 = f32[128,512]{1,0:T(8,128)} custom-call(f32[4,128,512]{2,1,0:T(8,128)} %convolution_bitcast_fusion.5.x_ref), custom_call_target="tpu_custom_call" | custom-call | tf_op jit(solution)/shard_map/pallas_call | solution.py:48
  67.2 2.1 convolution_convert_fusion.2
  69.3 12.3 %shard_map.79 = bf16[4,128,512]{2,1,0:T(8,128)(2,1)} custom-call(bf16[128,512]{1,0:T(8,128)(2,1)} %bitcast.110), custom_call_target="tpu_custom_call" | custom-call | tf_op jit(solution)/shard_map/pallas_call | solution.py:78
  81.6 2.4 %convolution_bitcast_fusion.1 = f32[4,128,512]{2,1,0:T(8,128)} fusion(bf16[6,4,4,128,128]{4,3,2,1,0:T(8,128)(2,1)S(1)} %bitcast_multiply_fusion, bf16[4,128,512]{2,1,0:T(8,128)(2,1)} %shard_map.79), kind=kOutput, calls=%fused_computation.2 | convolution fusion | flops 268435456 | bytes 2097152 | tf_op jit(solution)/shard_map/jznv,zvs->jns/dot_general | solution.py:183
  84.1 2.5 %convolution_bitcast_fusion.3 = f32[4,128,512]{2,1,0:T(8,128)} fusion(bf16[6,4,4,128,128]{4,3,2,1,0:T(8,128)(2,1)S(1)} %bitcast_multiply_fusion, bf16[4,128,512]{2,1,0:T(8,128)(2,1)} %shard_map.79), kind=kOutput, calls=%fused_computation.4 | convolution fusion | flops 268435456 | bytes 2097152 | tf_op jit(solution)/shard_map/jznv,zvs->jns/dot_general | solution.py:183
  86.6 0.7 reshape.71
  87.3 0.0 copy-start.4
  87.3 2.9 %fusion.x_ref = f32[4,128,512]{2,1,0:T(8,128)} fusion(f32[4,128,512]{2,1,0:T(8,128)} %convolution_bitcast_fusion.3, bf16[6,4,4,128,128]{4,3,2,1,0:T(8,128)(2,1)S(1)} %bitcast_multiply_fusion, bf16[4,128,512]{2,1,0:T(8,128)(2,1)} %shard_map.77), kind=kOutput, calls=%fused_computation.7 | convolution fusion | flops 268697600 | bytes 3145728 | tf_op jit(solution)/shard_map/jznv,zvs->jns/dot_general | solution.py:183
  90.2 28.7 %shard_map.80 = f32[128,512]{1,0:T(8,128)} custom-call(f32[4,128,512]{2,1,0:T(8,128)} %fusion.x_ref), custom_call_target="tpu_custom_call" | custom-call | tf_op jit(solution)/shard_map/pallas_call | solution.py:48
  118.9 0.0 copy-done.4
  118.9 2.0 convolution_convert_fusion.1
  121.0 10.0 %shard_map.81 = bf16[4,128,512]{2,1,0:T(8,128)(2,1)} custom-call(bf16[128,512]{1,0:T(8,128)(2,1)} %bitcast.112), custom_call_target="tpu_custom_call" | custom-call | tf_op jit(solution)/shard_map/pallas_call | solution.py:78
  131.0 1.5 convolution_bitcast_fusion
  132.5 0.0 copy-start.1
  132.5 0.0 copy-start.2
  132.5 2.8 %fusion.2.x_ref = f32[4,128,512]{2,1,0:T(8,128)} fusion(f32[4,128,512]{2,1,0:T(8,128)S(1)} %convolution_bitcast_fusion, f32[4,128,512]{2,1,0:T(8,128)} %convolution_bitcast_fusion.1, bf16[6,4,4,128,128]{4,3,2,1,0:T(8,128)(2,1)S(1)} %bitcast_multiply_fusion, bf16[4,128,512]{2,1,0:T(8,128)(2,1)} %shard_map.77), kind=kOutput, calls=%fused_computation.9 | convolution fusion | flops 268959744 | bytes 4194304 | tf_op jit(solution)/shard_map/jznv,zvs->jns/dot_general | solution.py:183
  135.3 0.0 copy-start.3
  135.3 28.6 %shard_map.82 = f32[128,512]{1,0:T(8,128)} custom-call(f32[4,128,512]{2,1,0:T(8,128)} %fusion.2.x_ref), custom_call_target="tpu_custom_call" | custom-call | tf_op jit(solution)/shard_map/pallas_call | solution.py:48
  163.9 1.7 reshape.66.x_ref
  165.6 38.5 %shard_map.83 = f32[32,16,128]{2,1,0:T(8,128)} custom-call(f32[32,16,128]{2,1,0:T(8,128)} %reshape.66.x_ref), custom_call_target="tpu_custom_call" | custom-call | tf_op jit(solution)/shard_map/pallas_call | solution.py:123
  204.1 1.1 sub.14
  205.2 0.0 copy-done
  205.2 0.4 convolution_convert_fusion
  205.6 0.0 copy-done.1
  205.6 0.0 copy-done.2
  205.7 0.0 copy-done.3
  205.7 0.1 pad_maximum_fusion.1
  205.7 23.9 %all_to_all.21 = bf16[4,4,32,512]{3,2,0,1:T(8,128)(2,1)S(1)} all-to-all(bf16[4,4,32,512]{3,2,0,1:T(8,128)(2,1)S(1)} %pad_maximum_fusion.1), channel_id=1, replica_groups=mesh['layer'=32,'prow'=4,'pcol'=4] {'pcol'}, dimensions={1} | all-to-all | bytes 1048576 | tf_op jit(solution)/shard_map/all_to_all | solution.py:205
  229.6 10.9 %all_to_all.22 = bf16[4,4,32,512]{3,2,0,1:T(8,128)(2,1)S(1)} all-to-all(bf16[4,4,32,512]{3,2,0,1:T(8,128)(2,1)S(1)} %all_to_all.21), channel_id=1, replica_groups=mesh['layer'=32,'prow'=4,'pcol'=4] {'prow'}, dimensions={1} | all-to-all | bytes 1048576 | tf_op jit(solution)/shard_map/all_to_all | solution.py:204
  240.6 0.8 copy.27
  241.4 0.7 slice.78
  (4 shorter events, 0.1 us)
Async XLA Ops:
  0.6 204.6 %copy-start = (f32[1,1,128,128]{3,2,1,0:T(8,128)S(1)}, f32[1,1,128,128]{3,2,1,0:T(8,128)}, u32[]{:S(2)}) copy-start(f32[1,1,128,128]{3,2,1,0:T(8,128)} %param.11) | copy-start | bytes 196612
  0.6 20.3 %copy-start.5 = (s32[1,6,1,1,4,4]{1,5,4,3,2,0:T(4,128)S(1)}, s32[1,6,1,1,4,4]{1,5,4,3,2,0:T(4,128)}, u32[]{:S(2)}) copy-start(s32[1,6,1,1,4,4]{1,5,4,3,2,0:T(4,128)} %param.9) | copy-start | bytes 1156
  16.8 15.4 %all-to-all-start.1 = ((bf16[4,4,32,512]{3,2,0,1:T(8,128)(2,1)}), bf16[4,4,32,512]{3,2,0,1:T(8,128)(2,1)}, u32[]{:S(2)}, u32[]{:S(2)}) async-start(bf16[4,4,32,512]{3,2,0,1:T(8,128)(2,1)} %all_to_all.20), calls=%async_computation.1 | async-start | bytes 1048576 | tf_op jit(solution)/shard_map/all_to_all | solution.py:149
  87.3 31.6 %copy-start.4 = (bf16[1,4,32,512]{3,2,0,1:T(8,128)(2,1)S(1)}, bf16[1,4,32,512]{3,2,0,1:T(8,128)(2,1)}, u32[]{:S(2)}) copy-start(bf16[1,4,32,512]{3,2,0,1:T(8,128)(2,1)} %get-tuple-element.2) | copy-start | bytes 393220
  132.5 73.2 %copy-start.1 = (bf16[512,128]{0,1:T(8,128)(2,1)S(1)}, bf16[512,128]{0,1:T(8,128)(2,1)}, u32[]{:S(2)}) copy-start(bf16[512,128]{0,1:T(8,128)(2,1)} %convolution_convert_fusion.3) | copy-start | bytes 393220
  132.5 73.2 %copy-start.2 = (bf16[512,128]{0,1:T(8,128)(2,1)S(1)}, bf16[512,128]{0,1:T(8,128)(2,1)}, u32[]{:S(2)}) copy-start(bf16[512,128]{0,1:T(8,128)(2,1)} %convolution_convert_fusion.2) | copy-start | bytes 393220
  135.3 70.3 %copy-start.3 = (bf16[512,128]{0,1:T(8,128)(2,1)S(1)}, bf16[512,128]{0,1:T(8,128)(2,1)}, u32[]{:S(2)}) copy-start(bf16[512,128]{0,1:T(8,128)(2,1)} %convolution_convert_fusion.1) | copy-start | bytes 393220

commit v2 on v1

--- a/solution.py
+++ b/solution.py
@@ -132,6 +132,72 @@
             pltpu.SemaphoreType.DMA((n - 1,)),
             pltpu.SemaphoreType.DMA((n - 1,)),
             pltpu.SemaphoreType.DMA((n - 1,)),
+        ],
+        compiler_params=_params(cid),
+    )(x)
+
+
+def permute_rows(x, forward, cid):
+    g = x.shape[1]
+
+    def kernel(x_ref, o_ref, ssem, rsem, lsem):
+        p = lax.axis_index("prow")
+        q = lax.axis_index("pcol")
+        barrier = pltpu.get_barrier_semaphore()
+        for dp in range(g):
+            for dq in range(g):
+                if dp or dq:
+                    pl.semaphore_signal(
+                        barrier, 1, device_id={"prow": (p + dp) % g, "pcol": (q + dq) % g},
+                        device_id_type=MESH)
+        pl.semaphore_wait(barrier, g * g - 1)
+        own = p == q
+        slot = q if forward else p
+        sends = []
+        for dj in range(g):
+            j = (p + dj) % g
+            dest = {"prow": j, "pcol": p} if forward else {"prow": q, "pcol": j}
+            copy = pltpu.make_async_remote_copy(
+                x_ref.at[:, j], o_ref.at[:, slot], ssem.at[dj], rsem.at[slot],
+                device_id=dest, device_id_type=MESH)
+            if dj == 0:
+                local = pltpu.make_async_copy(x_ref.at[:, j], o_ref.at[:, j], lsem)
+
+                @pl.when(own)
+                def _():
+                    local.start()
+
+                @pl.when(jnp.logical_not(own))
+                def _():
+                    copy.start()
+            else:
+                copy.start()
+            sends.append(copy)
+        for dj in range(g):
+            s = (p + dj) % g
+            arrival = pltpu.make_async_copy(x_ref.at[:, s], o_ref.at[:, s], rsem.at[s])
+            if dj == 0:
+                @pl.when(own)
+                def _():
+                    local.wait()
+
+                @pl.when(jnp.logical_not(own))
+                def _():
+                    sends[0].wait_send()
+                    arrival.wait()
+            else:
+                sends[dj].wait_send()
+                arrival.wait()
+
+    return pl.pallas_call(
+        kernel,
+        out_shape=jax.ShapeDtypeStruct(x.shape, x.dtype),
+        in_specs=[VMEM_SPEC],
+        out_specs=VMEM_SPEC,
+        scratch_shapes=[
+            pltpu.SemaphoreType.DMA((g,)),
+            pltpu.SemaphoreType.DMA((g,)),
+            pltpu.SemaphoreType.DMA(()),
         ],
         compiler_params=_params(cid),
     )(x)
@@ -146,13 +212,7 @@
     local_forest = subtree_right_hand.reshape(3, grid_size, slice_rows, rhs_cols)
     local_root = root_rhs.reshape(1, grid_size, slice_rows, rhs_cols)
     joined = jnp.concatenate([local_forest, local_root], axis=0)
-    placed = lax.all_to_all(
-        lax.all_to_all(joined, "prow", split_axis=1, concat_axis=1, tiled=True),
-        "pcol",
-        split_axis=1,
-        concat_axis=1,
-        tiled=True,
-    )
+    placed = permute_rows(joined, True, 40)
     placed = placed.reshape(4, super_rows, rhs_cols)
     block_mask = pattern.reshape(6, grid_size, grid_size).astype(jnp.bfloat16)
     masked = (
@@ -201,13 +261,7 @@
         preferred_element_type=jnp.float32,
     ).astype(jnp.bfloat16)
     stacked = jnp.stack(solved + [root_answer]).reshape(4, grid_size, slice_rows, rhs_cols)
-    returned = lax.all_to_all(
-        lax.all_to_all(stacked, "pcol", split_axis=1, concat_axis=1, tiled=True),
-        "prow",
-        split_axis=1,
-        concat_axis=1,
-        tiled=True,
-    )
+    returned = permute_rows(stacked, False, 41)
     forest_out = returned[:3].reshape(1, 3 * super_rows, rhs_cols)
     root_out = returned[3].reshape(super_rows, rhs_cols)
     return (forest_out, root_out)

time: 244 us -> 250 us (1.025)
  Pallas kernels: 147 us -> 216 us
  blocking collectives: 49.8 us -> 0 us
  waiting for transfers between devices: 8.95 us -> 0 us
  starting transfers between devices: 4.14 us -> 0 us
  matrix products: 20.8 us -> 17.4 us
    pallas_call x0 -> x2, Pallas kernels: none -> 68.9 us  [permute_rows(): pl.pallas_call(kernel, out_shape=jax.ShapeDtypeStruct(x.shape, x.dtype),...]
    all_to_all x3 -> x0, blocking collectives: 49.8 us -> none  [the longest x1 23.9 us: shards(): lax.all_to_all(stacked, 'pcol', split_axis=1, concat_axis=1, tiled=True)]
    all_to_all x1 -> x0, waiting for transfers between devices: 8.95 us -> none  [shards(): lax.all_to_all(lax.all_to_all(joined, 'prow', split_axis=1, concat_axis=1...]
    pallas_call x3, Pallas kernels: 76.3 us -> 80.6 us  [reduce_scatter(): pl.pallas_call(kernel, out_shape=jax.ShapeDtypeStruct(x.shape[1:], x.dtyp...]
    all_to_all x1 -> x0, starting transfers between devices: 4.14 us -> none  [shards(): lax.all_to_all(lax.all_to_all(joined, 'prow', split_axis=1, concat_axis=1...]
    pallas_call x1, Pallas kernels: 38.5 us -> 34.5 us  [all_reduce(): pl.pallas_call(kernel, out_shape=jax.ShapeDtypeStruct(x.shape, x.dtype),...]
    dot_general x6, matrix products: 14.6 us -> 11.2 us  [shards(): jnp.einsum('jznv,zvs->jns', factor_weights, block_pieces, preferred_eleme...]
  transfers between devices with their start and end apart: 1 -> 0, of which waited for: 1 -> 0; matrix products, arithmetic and copies ran while one was open for 1% -> 0% of each run, Pallas kernels for 0% -> 0%
where the time goes in v2:
time: 250 us; the launch traced here: 248 us
  Pallas kernels  216 us (86%)
  matrix products  17.4 us (7%)
  other arithmetic  7.93 us (3%)
  local copies, waits for them, and re-layouts  5.92 us (2%)
    pallas_call x3, Pallas kernels, reduce_scatter(): pl.pallas_call(kernel, out_shape=jax.ShapeDtypeStruct(x.shape[1:], x.dtyp...  80.6 us
    pallas_call x2, Pallas kernels, permute_rows(): pl.pallas_call(kernel, out_shape=jax.ShapeDtypeStruct(x.shape, x.dtype),...  68.9 us
    pallas_call x1, Pallas kernels, all_reduce(): pl.pallas_call(kernel, out_shape=jax.ShapeDtypeStruct(x.shape, x.dtype),...  34.5 us
    pallas_call x3, Pallas kernels, all_gather(): pl.pallas_call(kernel, out_shape=jax.ShapeDtypeStruct((n,) + x.shape, x.d...  31.9 us
    dot_general x6, matrix products, shards(): jnp.einsum('jznv,zvs->jns', factor_weights, block_pieces, preferred_eleme...  11.2 us
    dot_general x3, matrix products, shards(): jnp.dot(inverses[tier_index], right_hand_side, precision=lax.Precision.HI...  5.79 us

profile of v2, /device:TPU:6, one launch (start us, length us, event | category | flops | bytes accessed | tf_op | source)
XLA Modules:
  0.0 248.0 jit_solution(2848882085895184451)
XLA Ops:
  0.6 0.0 copy-start
  0.6 0.7 convert_bitcast_fusion
  1.4 0.1 copy.8
  1.5 1.9 pad_maximum_fusion.x_ref
  3.4 43.3 %shard_map.77 = bf16[4,4,32,512]{3,2,1,0:T(8,128)(2,1)} custom-call(bf16[4,4,32,512]{3,2,1,0:T(8,128)(2,1)} %pad_maximum_fusion.x_ref), custom_call_target="tpu_custom_call" | custom-call | tf_op jit(solution)/shard_map/pallas_call | solution.py:192
  46.7 1.1 fusion.16
  47.8 1.8 convolution_convert_fusion.3
  49.6 0.7 reshape.71
  50.3 11.9 %shard_map.78 = bf16[4,128,512]{2,1,0:T(8,128)(2,1)} custom-call(bf16[128,512]{1,0:T(8,128)(2,1)} %bitcast.98), custom_call_target="tpu_custom_call" | custom-call | tf_op jit(solution)/shard_map/pallas_call | solution.py:78
  62.2 0.0 copy-start.1
  62.2 2.2 bitcast_multiply_fusion
  64.4 0.0 copy-done.1
  64.4 1.4 convolution_bitcast_fusion.5.x_ref
  65.9 23.9 %shard_map.79 = f32[128,512]{1,0:T(8,128)} custom-call(f32[4,128,512]{2,1,0:T(8,128)} %convolution_bitcast_fusion.5.x_ref), custom_call_target="tpu_custom_call" | custom-call | tf_op jit(solution)/shard_map/pallas_call | solution.py:48
  89.7 2.0 convolution_convert_fusion.2
  91.8 10.0 %shard_map.80 = bf16[4,128,512]{2,1,0:T(8,128)(2,1)} custom-call(bf16[128,512]{1,0:T(8,128)(2,1)} %bitcast.100), custom_call_target="tpu_custom_call" | custom-call | tf_op jit(solution)/shard_map/pallas_call | solution.py:78
  101.8 0.0 copy-start.2
  101.8 2.5 %convolution_bitcast_fusion.1 = f32[4,128,512]{2,1,0:T(8,128)} fusion(bf16[6,4,4,128,128]{4,3,2,1,0:T(8,128)(2,1)S(1)} %bitcast_multiply_fusion, bf16[4,128,512]{2,1,0:T(8,128)(2,1)} %shard_map.80), kind=kOutput, calls=%fused_computation.2 | convolution fusion | flops 268435456 | bytes 2097152 | tf_op jit(solution)/shard_map/jznv,zvs->jns/dot_general | solution.py:243
  104.3 1.5 convolution_bitcast_fusion.3
  105.8 0.0 copy-done.2
  105.8 1.5 fusion.x_ref
  107.3 28.3 %shard_map.81 = f32[128,512]{1,0:T(8,128)} custom-call(f32[4,128,512]{2,1,0:T(8,128)} %fusion.x_ref), custom_call_target="tpu_custom_call" | custom-call | tf_op jit(solution)/shard_map/pallas_call | solution.py:48
  135.6 2.0 convolution_convert_fusion.1
  137.6 10.0 %shard_map.82 = bf16[4,128,512]{2,1,0:T(8,128)(2,1)} custom-call(bf16[128,512]{1,0:T(8,128)(2,1)} %bitcast.102), custom_call_target="tpu_custom_call" | custom-call | tf_op jit(solution)/shard_map/pallas_call | solution.py:78
  147.7 1.5 convolution_bitcast_fusion
  149.1 0.0 copy-start.3
  149.1 0.0 copy-start.4
  149.2 2.8 %fusion.2.x_ref = f32[4,128,512]{2,1,0:T(8,128)} fusion(f32[4,128,512]{2,1,0:T(8,128)S(1)} %convolution_bitcast_fusion, f32[4,128,512]{2,1,0:T(8,128)} %convolution_bitcast_fusion.1, bf16[6,4,4,128,128]{4,3,2,1,0:T(8,128)(2,1)S(1)} %bitcast_multiply_fusion, bf16[4,128,512]{2,1,0:T(8,128)(2,1)} %shard_map.78), kind=kOutput, calls=%fused_computation.9 | convolution fusion | flops 268959744 | bytes 4194304 | tf_op jit(solution)/shard_map/jznv,zvs->jns/dot_general | solution.py:243
  152.0 0.0 copy-start.5
  152.0 28.4 %shard_map.83 = f32[128,512]{1,0:T(8,128)} custom-call(f32[4,128,512]{2,1,0:T(8,128)} %fusion.2.x_ref), custom_call_target="tpu_custom_call" | custom-call | tf_op jit(solution)/shard_map/pallas_call | solution.py:48
  180.4 1.7 reshape.66.x_ref
  182.1 34.5 %shard_map.84 = f32[32,16,128]{2,1,0:T(8,128)} custom-call(f32[32,16,128]{2,1,0:T(8,128)} %reshape.66.x_ref), custom_call_target="tpu_custom_call" | custom-call | tf_op jit(solution)/shard_map/pallas_call | solution.py:123
  216.6 1.1 sub.14
  217.7 0.0 copy-done
  217.7 0.4 convolution_convert_fusion
  218.1 0.0 copy-done.3
  218.1 0.0 copy-done.4
  218.1 0.0 copy-done.5
  218.1 0.9 pad_maximum_fusion.1.x_ref
  219.0 25.6 %shard_map.85 = bf16[4,4,32,512]{3,2,1,0:T(8,128)(2,1)} custom-call(bf16[4,4,32,512]{3,2,1,0:T(8,128)(2,1)} %pad_maximum_fusion.1.x_ref), custom_call_target="tpu_custom_call" | custom-call | tf_op jit(solution)/shard_map/pallas_call | solution.py:192
  244.6 1.6 slice.66
  246.2 1.8 slice.65
  (1 shorter events, 0.0 us)
Async XLA Ops:
  0.6 217.0 %copy-start = (f32[1,1,128,128]{3,2,1,0:T(8,128)S(1)}, f32[1,1,128,128]{3,2,1,0:T(8,128)}, u32[]{:S(2)}) copy-start(f32[1,1,128,128]{3,2,1,0:T(8,128)} %param.11) | copy-start | bytes 196612
  62.2 2.2 copy-start.1
  101.8 4.0 %copy-start.2 = (bf16[4,128,512]{2,1,0:T(8,128)(2,1)S(1)}, bf16[4,128,512]{2,1,0:T(8,128)(2,1)}, u32[]{:S(2)}) copy-start(bf16[4,128,512]{2,1,0:T(8,128)(2,1)} %shard_map.78) | copy-start | bytes 1572868
  149.1 68.9 %copy-start.3 = (bf16[512,128]{0,1:T(8,128)(2,1)S(1)}, bf16[512,128]{0,1:T(8,128)(2,1)}, u32[]{:S(2)}) copy-start(bf16[512,128]{0,1:T(8,128)(2,1)} %convolution_convert_fusion.3) | copy-start | bytes 393220
  149.1 68.9 %copy-start.4 = (bf16[512,128]{0,1:T(8,128)(2,1)S(1)}, bf16[512,128]{0,1:T(8,128)(2,1)}, u32[]{:S(2)}) copy-start(bf16[512,128]{0,1:T(8,128)(2,1)} %convolution_convert_fusion.2) | copy-start | bytes 393220
  152.0 66.1 %copy-start.5 = (bf16[512,128]{0,1:T(8,128)(2,1)S(1)}, bf16[512,128]{0,1:T(8,128)(2,1)}, u32[]{:S(2)}) copy-start(bf16[512,128]{0,1:T(8,128)(2,1)} %convolution_convert_fusion.1) | copy-start | bytes 393220

commit v3 on v2

--- a/solution.py
+++ b/solution.py
@@ -24,10 +24,10 @@
     return pltpu.CompilerParams(collective_id=cid, has_side_effects=True)
 
 
-def reduce_scatter(x, axis, cid):
+def reduce_scatter(x, own_part, axis, cid, wire):
     n = x.shape[0]
 
-    def kernel(x_ref, o_ref, recv, ssem, rsem):
+    def kernel(x_ref, own_ref, o_ref, recv, ssem, rsem):
         me = lax.axis_index(axis)
         _barrier(axis, n, me)
         copies = []
@@ -40,23 +40,23 @@
             copies.append(copy)
         for copy in copies:
             copy.wait()
-        total = x_ref[me]
+        total = own_ref[...]
         for d in range(n - 1):
-            total = total + recv[d]
+            total = total + recv[d].astype(jnp.float32)
         o_ref[...] = total
 
     return pl.pallas_call(
         kernel,
-        out_shape=jax.ShapeDtypeStruct(x.shape[1:], x.dtype),
-        in_specs=[VMEM_SPEC],
-        out_specs=VMEM_SPEC,
-        scratch_shapes=[
-            pltpu.VMEM((n - 1,) + x.shape[1:], x.dtype),
-            pltpu.SemaphoreType.DMA((n - 1,)),
-            pltpu.SemaphoreType.DMA((n - 1,)),
-        ],
-        compiler_params=_params(cid),
-    )(x)
+        out_shape=jax.ShapeDtypeStruct(x.shape[1:], jnp.float32),
+        in_specs=[VMEM_SPEC, VMEM_SPEC],
+        out_specs=VMEM_SPEC,
+        scratch_shapes=[
+            pltpu.VMEM((n - 1,) + x.shape[1:], wire),
+            pltpu.SemaphoreType.DMA((n - 1,)),
+            pltpu.SemaphoreType.DMA((n - 1,)),
+        ],
+        compiler_params=_params(cid),
+    )(x, own_part)
 
 
 def all_gather(x, axis, n, cid):
@@ -226,7 +226,9 @@
     for tier_index in range(3):
         right_hand_side = placed[tier_index].astype(jnp.float32)
         if tier_index > 0:
-            reduced = reduce_scatter(totals[tier_index], "pcol", 10 + tier_index)
+            rows = totals[tier_index]
+            own_rows = rows[lax.axis_index("pcol")]
+            reduced = reduce_scatter(rows.astype(jnp.bfloat16), own_rows, "pcol", 10 + tier_index, jnp.bfloat16)
             right_hand_side = right_hand_side - reduced
         answer = jnp.dot(
             inverses[tier_index],
@@ -250,7 +252,7 @@
             else:
                 updated_rows.append(totals[target])
         totals = tuple(updated_rows)
-    row_share = reduce_scatter(totals[3], "pcol", 13)
+    row_share = reduce_scatter(totals[3], totals[3][lax.axis_index("pcol")], "pcol", 13, jnp.float32)
     chunks = row_share.reshape(n_layer, -1, 128)
     reduced_root = all_reduce(chunks, "layer", 30).reshape(super_rows, rhs_cols)
     root_side = placed[3].astype(jnp.float32) - reduced_root

time: 250 us -> 229 us (0.916)
  Pallas kernels: 216 us -> 193 us
  local copies, waits for them, and re-layouts: 5.92 us -> 9.3 us
    pallas_call x3, Pallas kernels: 80.6 us -> 57.8 us  [reduce_scatter(): pl.pallas_call(kernel, out_shape=jax.ShapeDtypeStruct(x.shape[1:], jnp.fl...]
    squeeze x0 -> x3, local copies, waits for them, and re-layouts: none -> 3.11 us  [the longest x2 2.39 us: shards(): own_rows = rows[lax.axis_index('pcol')]]
where the time goes in v3:
time: 229 us; the launch traced here: 227 us
  Pallas kernels  193 us (84%)
  matrix products  16.1 us (7%)
  local copies, waits for them, and re-layouts  9.3 us (4%)
  other arithmetic  7.82 us (3%)
    pallas_call x2, Pallas kernels, permute_rows(): pl.pallas_call(kernel, out_shape=jax.ShapeDtypeStruct(x.shape, x.dtype),...  68.4 us
    pallas_call x3, Pallas kernels, reduce_scatter(): pl.pallas_call(kernel, out_shape=jax.ShapeDtypeStruct(x.shape[1:], jnp.fl...  57.8 us
    pallas_call x1, Pallas kernels, all_reduce(): pl.pallas_call(kernel, out_shape=jax.ShapeDtypeStruct(x.shape, x.dtype),...  34.5 us
    pallas_call x3, Pallas kernels, all_gather(): pl.pallas_call(kernel, out_shape=jax.ShapeDtypeStruct((n,) + x.shape, x.d...  31.9 us
    dot_general x6, matrix products, shards(): jnp.einsum('jznv,zvs->jns', factor_weights, block_pieces, preferred_eleme...  9.81 us
    dot_general x3, matrix products, shards(): jnp.dot(inverses[tier_index], right_hand_side, precision=lax.Precision.HI...  5.93 us

profile of v3, /device:TPU:6, one launch (start us, length us, event | category | flops | bytes accessed | tf_op | source)
XLA Modules:
  0.0 226.7 jit_solution(9399238363512530299)
XLA Ops:
  0.6 0.0 copy-start
  0.6 0.0 copy-start.7
  0.7 1.9 pad_maximum_fusion.x_ref
  2.6 43.3 %shard_map.77 = bf16[4,4,32,512]{3,2,1,0:T(8,128)(2,1)} custom-call(bf16[4,4,32,512]{3,2,1,0:T(8,128)(2,1)} %pad_maximum_fusion.x_ref), custom_call_target="tpu_custom_call" | custom-call | tf_op jit(solution)/shard_map/pallas_call | solution.py:192
  45.8 1.8 fusion.16
  47.7 0.0 copy-done.7
  47.7 0.1 copy.8
  47.9 0.0 copy-start.6
  47.9 2.2 bitcast_multiply_fusion
  50.1 0.0 copy-done.6
  50.1 1.8 convolution_convert_fusion.3
  51.8 11.9 %shard_map.78 = bf16[4,128,512]{2,1,0:T(8,128)(2,1)} custom-call(bf16[128,512]{1,0:T(8,128)(2,1)} %bitcast.112), custom_call_target="tpu_custom_call" | custom-call | tf_op jit(solution)/shard_map/pallas_call | solution.py:78
  63.8 2.6 %fusion.17 = (bf16[4,128,512]{2,1,0:T(8,128)(2,1)}, f32[4,128,512]{2,1,0:T(8,128)}) fusion(bf16[4,128,512]{2,1,0:T(8,128)(2,1)} %shard_map.78, bf16[6,4,4,128,128]{4,3,2,1,0:T(8,128)(2,1)S(1)} %bitcast_multiply_fusion), kind=kOutput, calls=%fused_computation.43 | convolution fusion | flops 268697600 | bytes 2621440 | tf_op jit(solution)/shard_map/jznv,zvs->jns/dot_general | solution.py:245
  66.4 1.7 dynamic-slice_bitcast_fusion.2.own_ref
  68.1 15.3 %shard_map.79 = f32[128,512]{1,0:T(8,128)} custom-call(bf16[4,128,512]{2,1,0:T(8,128)(2,1)} %get-tuple-element.6.x_ref, f32[128,512]{1,0:T(8,128)} %dynamic-slice_bitcast_fusion.2.own_ref), custom_call_target="tpu_custom_call" | custom-call | tf_op jit(solution)/shard_map/pallas_call | solution.py:48
  83.4 2.1 convolution_convert_fusion.2
  85.5 10.0 %shard_map.80 = bf16[4,128,512]{2,1,0:T(8,128)(2,1)} custom-call(bf16[128,512]{1,0:T(8,128)(2,1)} %bitcast.114), custom_call_target="tpu_custom_call" | custom-call | tf_op jit(solution)/shard_map/pallas_call | solution.py:78
  95.5 1.5 convolution_bitcast_fusion.3
  97.0 2.3 fusion.18
  99.2 0.7 dynamic-slice_bitcast_fusion.1.own_ref
  100.0 17.0 %shard_map.81 = f32[128,512]{1,0:T(8,128)} custom-call(bf16[4,128,512]{2,1,0:T(8,128)(2,1)} %get-tuple-element.8.x_ref, f32[128,512]{1,0:T(8,128)} %dynamic-slice_bitcast_fusion.1.own_ref), custom_call_target="tpu_custom_call" | custom-call | tf_op jit(solution)/shard_map/pallas_call | solution.py:48
  117.0 2.1 convolution_convert_fusion.1
  119.1 10.0 %shard_map.82 = bf16[4,128,512]{2,1,0:T(8,128)(2,1)} custom-call(bf16[128,512]{1,0:T(8,128)(2,1)} %bitcast.116), custom_call_target="tpu_custom_call" | custom-call | tf_op jit(solution)/shard_map/pallas_call | solution.py:78
  129.1 0.0 copy-start.1
  129.1 1.5 convolution_bitcast_fusion
  130.6 1.5 convolution_bitcast_fusion.1
  132.1 0.0 copy-done.1
  132.1 0.4 fusion.2.x_ref
  132.5 0.0 copy-start.2
  132.6 1.0 copy-done.2
  133.5 0.0 copy-start.3
  133.5 0.0 copy-start.4
  133.5 0.0 copy-start.5
  133.5 0.7 dynamic-slice_bitcast_fusion.own_ref
  134.2 25.5 %shard_map.83 = f32[128,512]{1,0:T(8,128)} custom-call(f32[4,128,512]{2,1,0:T(8,128)} %copy-done.2, f32[128,512]{1,0:T(8,128)} %dynamic-slice_bitcast_fusion.own_ref), custom_call_target="tpu_custom_call" | custom-call | tf_op jit(solution)/shard_map/pallas_call | solution.py:48
  159.8 1.7 reshape.66.x_ref
  161.4 34.5 %shard_map.84 = f32[32,16,128]{2,1,0:T(8,128)} custom-call(f32[32,16,128]{2,1,0:T(8,128)} %reshape.66.x_ref), custom_call_target="tpu_custom_call" | custom-call | tf_op jit(solution)/shard_map/pallas_call | solution.py:123
  195.9 1.0 sub.14
  196.9 0.0 copy-done
  197.0 0.4 convolution_convert_fusion
  197.4 0.0 copy-done.3
  197.4 0.0 copy-done.4
  197.4 0.0 copy-done.5
  197.4 0.9 pad_maximum_fusion.1.x_ref
  198.3 25.1 %shard_map.85 = bf16[4,4,32,512]{3,2,1,0:T(8,128)(2,1)} custom-call(bf16[4,4,32,512]{3,2,1,0:T(8,128)(2,1)} %pad_maximum_fusion.1.x_ref), custom_call_target="tpu_custom_call" | custom-call | tf_op jit(solution)/shard_map/pallas_call | solution.py:192
  223.4 1.8 slice.65
  225.2 1.6 slice.66
  (3 shorter events, 0.1 us)
Async XLA Ops:
  0.6 196.3 %copy-start = (f32[1,1,128,128]{3,2,1,0:T(8,128)S(1)}, f32[1,1,128,128]{3,2,1,0:T(8,128)}, u32[]{:S(2)}) copy-start(f32[1,1,128,128]{3,2,1,0:T(8,128)} %param.11) | copy-start | bytes 196612
  0.6 47.1 %copy-start.7 = (s32[1,6,1,1,4,4]{1,5,4,3,2,0:T(4,128)S(1)}, s32[1,6,1,1,4,4]{1,5,4,3,2,0:T(4,128)}, u32[]{:S(2)}) copy-start(s32[1,6,1,1,4,4]{1,5,4,3,2,0:T(4,128)} %param.9) | copy-start | bytes 1156
  47.9 2.2 copy-start.6
  129.1 3.0 %copy-start.1 = (bf16[4,128,512]{2,1,0:T(8,128)(2,1)S(1)}, bf16[4,128,512]{2,1,0:T(8,128)(2,1)}, u32[]{:S(2)}) copy-start(bf16[4,128,512]{2,1,0:T(8,128)(2,1)} %shard_map.78) | copy-start | bytes 1572868
  132.5 1.0 copy-start.2
  133.5 63.8 %copy-start.3 = (bf16[512,128]{0,1:T(8,128)(2,1)S(1)}, bf16[512,128]{0,1:T(8,128)(2,1)}, u32[]{:S(2)}) copy-start(bf16[512,128]{0,1:T(8,128)(2,1)} %convolution_convert_fusion.3) | copy-start | bytes 393220
  133.5 63.9 %copy-start.4 = (bf16[512,128]{0,1:T(8,128)(2,1)S(1)}, bf16[512,128]{0,1:T(8,128)(2,1)}, u32[]{:S(2)}) copy-start(bf16[512,128]{0,1:T(8,128)(2,1)} %convolution_convert_fusion.2) | copy-start | bytes 393220
  133.5 63.9 %copy-start.5 = (bf16[512,128]{0,1:T(8,128)(2,1)S(1)}, bf16[512,128]{0,1:T(8,128)(2,1)}, u32[]{:S(2)}) copy-start(bf16[512,128]{0,1:T(8,128)(2,1)} %convolution_convert_fusion.1) | copy-start | bytes 393220

commit v4 on v3

--- a/solution.py
+++ b/solution.py
@@ -137,42 +137,42 @@
     )(x)
 
 
-def permute_rows(x, forward, cid):
-    g = x.shape[1]
-
-    def kernel(x_ref, o_ref, ssem, rsem, lsem):
-        p = lax.axis_index("prow")
-        q = lax.axis_index("pcol")
-        barrier = pltpu.get_barrier_semaphore()
-        for dp in range(g):
-            for dq in range(g):
-                if dp or dq:
-                    pl.semaphore_signal(
-                        barrier, 1, device_id={"prow": (p + dp) % g, "pcol": (q + dq) % g},
-                        device_id_type=MESH)
-        pl.semaphore_wait(barrier, g * g - 1)
-        own = p == q
-        slot = q if forward else p
-        sends = []
-        for dj in range(g):
-            j = (p + dj) % g
-            dest = {"prow": j, "pcol": p} if forward else {"prow": q, "pcol": j}
-            copy = pltpu.make_async_remote_copy(
-                x_ref.at[:, j], o_ref.at[:, slot], ssem.at[dj], rsem.at[slot],
-                device_id=dest, device_id_type=MESH)
-            if dj == 0:
-                local = pltpu.make_async_copy(x_ref.at[:, j], o_ref.at[:, j], lsem)
-
-                @pl.when(own)
-                def _():
-                    local.start()
-
-                @pl.when(jnp.logical_not(own))
-                def _():
-                    copy.start()
-            else:
+def _grid_barrier_signals(barrier, g, p, q):
+    for dp in range(g):
+        for dq in range(g):
+            if dp or dq:
+                pl.semaphore_signal(
+                    barrier, 1, device_id={"prow": (p + dp) % g, "pcol": (q + dq) % g},
+                    device_id_type=MESH)
+
+
+def _permute_start(x_ref, o_ref, forward, ssem, rsem, lsem):
+    g = x_ref.shape[1]
+    p = lax.axis_index("prow")
+    q = lax.axis_index("pcol")
+    own = p == q
+    slot = q if forward else p
+    sends = []
+    local = pltpu.make_async_copy(x_ref.at[:, p], o_ref.at[:, p], lsem)
+    for dj in range(g):
+        j = (p + dj) % g
+        dest = {"prow": j, "pcol": p} if forward else {"prow": q, "pcol": j}
+        copy = pltpu.make_async_remote_copy(
+            x_ref.at[:, j], o_ref.at[:, slot], ssem.at[dj], rsem.at[slot],
+            device_id=dest, device_id_type=MESH)
+        if dj == 0:
+            @pl.when(own)
+            def _():
+                local.start()
+
+            @pl.when(jnp.logical_not(own))
+            def _():
                 copy.start()
-            sends.append(copy)
+        else:
+            copy.start()
+        sends.append(copy)
+
+    def wait():
         for dj in range(g):
             s = (p + dj) % g
             arrival = pltpu.make_async_copy(x_ref.at[:, s], o_ref.at[:, s], rsem.at[s])
@@ -189,18 +189,98 @@
                 sends[dj].wait_send()
                 arrival.wait()
 
+    return wait
+
+
+def _permute_scratch(g):
+    return [pltpu.SemaphoreType.DMA((g,)), pltpu.SemaphoreType.DMA((g,)), pltpu.SemaphoreType.DMA(())]
+
+
+def permute_rows(x, forward, cid):
+    g = x.shape[1]
+
+    def kernel(x_ref, o_ref, ssem, rsem, lsem):
+        p = lax.axis_index("prow")
+        q = lax.axis_index("pcol")
+        barrier = pltpu.get_barrier_semaphore()
+        _grid_barrier_signals(barrier, g, p, q)
+        pl.semaphore_wait(barrier, g * g - 1)
+        _permute_start(x_ref, o_ref, forward, ssem, rsem, lsem)()
+
     return pl.pallas_call(
         kernel,
         out_shape=jax.ShapeDtypeStruct(x.shape, x.dtype),
         in_specs=[VMEM_SPEC],
         out_specs=VMEM_SPEC,
+        scratch_shapes=_permute_scratch(g),
+        compiler_params=_params(cid),
+    )(x)
+
+
+def root_exchange(chunks, forest, root_in, cid):
+    n = chunks.shape[0]
+    g = forest.shape[1]
+    axis = "layer"
+
+    def kernel(x_ref, f_ref, r_ref, o_ref, fo_ref, ro_ref, recv, part,
+               ssem, rsem, gsem, hsem, fs, fr, fl, rs, rr, rl):
+        me = lax.axis_index(axis)
+        p = lax.axis_index("prow")
+        q = lax.axis_index("pcol")
+        barrier = pltpu.get_barrier_semaphore()
+        for d in range(1, n):
+            pl.semaphore_signal(barrier, 1, device_id={axis: (me + d) % n}, device_id_type=MESH)
+        _grid_barrier_signals(barrier, g, p, q)
+        pl.semaphore_wait(barrier, n - 1 + g * g - 1)
+        root_wait = _permute_start(r_ref, ro_ref, True, rs, rr, rl)
+        forest_wait = _permute_start(f_ref, fo_ref, False, fs, fr, fl)
+        copies = []
+        for d in range(1, n):
+            peer = (me + d) % n
+            copy = pltpu.make_async_remote_copy(
+                x_ref.at[peer], recv.at[d - 1], ssem.at[d - 1], rsem.at[d - 1],
+                device_id={axis: peer}, device_id_type=MESH)
+            copy.start()
+            copies.append(copy)
+        for copy in copies:
+            copy.wait()
+        total = x_ref[me]
+        for d in range(n - 1):
+            total = total + recv[d]
+        part[...] = total
+        o_ref[me] = total
+        copies = []
+        for d in range(1, n):
+            peer = (me + d) % n
+            copy = pltpu.make_async_remote_copy(
+                part, o_ref.at[me], gsem.at[d - 1], hsem.at[d - 1],
+                device_id={axis: peer}, device_id_type=MESH)
+            copy.start()
+            copies.append(copy)
+        for copy in copies:
+            copy.wait()
+        root_wait()
+        forest_wait()
+
+    return pl.pallas_call(
+        kernel,
+        out_shape=(
+            jax.ShapeDtypeStruct(chunks.shape, chunks.dtype),
+            jax.ShapeDtypeStruct(forest.shape, forest.dtype),
+            jax.ShapeDtypeStruct(root_in.shape, root_in.dtype),
+        ),
+        in_specs=[VMEM_SPEC] * 3,
+        out_specs=(VMEM_SPEC,) * 3,
         scratch_shapes=[
-            pltpu.SemaphoreType.DMA((g,)),
-            pltpu.SemaphoreType.DMA((g,)),
-            pltpu.SemaphoreType.DMA(()),
-        ],
-        compiler_params=_params(cid),
-    )(x)
+            pltpu.VMEM((n - 1,) + chunks.shape[1:], chunks.dtype),
+            pltpu.VMEM(chunks.shape[1:], chunks.dtype),
+            pltpu.SemaphoreType.DMA((n - 1,)),
+            pltpu.SemaphoreType.DMA((n - 1,)),
+            pltpu.SemaphoreType.DMA((n - 1,)),
+            pltpu.SemaphoreType.DMA((n - 1,)),
+        ] + _permute_scratch(g) + _permute_scratch(g),
+        compiler_params=_params(cid),
+    )(chunks, forest, root_in)
 
 
 def shards(subtree_right_hand, root_rhs, blocks, pattern, forest_inverse, root_inverse):
@@ -211,9 +291,8 @@
     slice_rows = super_rows // grid_size
     local_forest = subtree_right_hand.reshape(3, grid_size, slice_rows, rhs_cols)
     local_root = root_rhs.reshape(1, grid_size, slice_rows, rhs_cols)
-    joined = jnp.concatenate([local_forest, local_root], axis=0)
-    placed = permute_rows(joined, True, 40)
-    placed = placed.reshape(4, super_rows, rhs_cols)
+    placed = permute_rows(local_forest, True, 40)
+    placed = placed.reshape(3, super_rows, rhs_cols)
     block_mask = pattern.reshape(6, grid_size, grid_size).astype(jnp.bfloat16)
     masked = (
         blocks.reshape(6, grid_size, grid_size, super_rows, super_rows)
@@ -254,18 +333,19 @@
         totals = tuple(updated_rows)
     row_share = reduce_scatter(totals[3], totals[3][lax.axis_index("pcol")], "pcol", 13, jnp.float32)
     chunks = row_share.reshape(n_layer, -1, 128)
-    reduced_root = all_reduce(chunks, "layer", 30).reshape(super_rows, rhs_cols)
-    root_side = placed[3].astype(jnp.float32) - reduced_root
+    forest_solved = jnp.stack(solved).reshape(3, grid_size, slice_rows, rhs_cols)
+    reduced_root, forest_back, root_placed = root_exchange(chunks, forest_solved, local_root, 30)
+    reduced_root = reduced_root.reshape(super_rows, rhs_cols)
+    root_side = root_placed.reshape(super_rows, rhs_cols).astype(jnp.float32) - reduced_root
     root_answer = jnp.dot(
         root_inverse.reshape(super_rows, super_rows),
         root_side,
         precision=lax.Precision.HIGHEST,
         preferred_element_type=jnp.float32,
     ).astype(jnp.bfloat16)
-    stacked = jnp.stack(solved + [root_answer]).reshape(4, grid_size, slice_rows, rhs_cols)
-    returned = permute_rows(stacked, False, 41)
-    forest_out = returned[:3].reshape(1, 3 * super_rows, rhs_cols)
-    root_out = returned[3].reshape(super_rows, rhs_cols)
+    root_back = permute_rows(root_answer.reshape(1, grid_size, slice_rows, rhs_cols), False, 41)
+    forest_out = forest_back.reshape(1, 3 * super_rows, rhs_cols)
+    root_out = root_back.reshape(super_rows, rhs_cols)
     return (forest_out, root_out)
 
 

time: 229 us -> 224 us (0.978)
  other arithmetic: 7.82 us -> 4.71 us
  Pallas kernels: 193 us -> 190 us
  local copies, waits for them, and re-layouts: 9.3 us -> 12 us
    pallas_call x2, Pallas kernels: 68.4 us -> 56.5 us  [permute_rows(): pl.pallas_call(kernel, out_shape=jax.ShapeDtypeStruct(x.shape, x.dtype),...]
    pallas_call x1, Pallas kernels: 34.5 us -> 44.1 us  [root_exchange(): pl.pallas_call(kernel, out_shape=(jax.ShapeDtypeStruct(chunks.shape, chun...]
    unnamed x16, local copies, waits for them, and re-layouts: 1 us -> 4.33 us
where the time goes in v4:
time: 224 us; the launch traced here: 223 us
  Pallas kernels  190 us (85%)
  matrix products  15.2 us (7%)
  local copies, waits for them, and re-layouts  12 us (5%)
  other arithmetic  4.71 us (2%)
    pallas_call x3, Pallas kernels, reduce_scatter(): pl.pallas_call(kernel, out_shape=jax.ShapeDtypeStruct(x.shape[1:], jnp.fl...  57.8 us
    pallas_call x2, Pallas kernels, permute_rows(): pl.pallas_call(kernel, out_shape=jax.ShapeDtypeStruct(x.shape, x.dtype),...  56.5 us
    pallas_call x1, Pallas kernels, root_exchange(): pl.pallas_call(kernel, out_shape=(jax.ShapeDtypeStruct(chunks.shape, chun...  44.1 us
    pallas_call x3, Pallas kernels, all_gather(): pl.pallas_call(kernel, out_shape=jax.ShapeDtypeStruct((n,) + x.shape, x.d...  31.9 us
    dot_general x6, matrix products, shards(): jnp.einsum('jznv,zvs->jns', factor_weights, block_pieces, preferred_eleme...  9.85 us

profile of v4, /device:TPU:6, one launch (start us, length us, event | category | flops | bytes accessed | tf_op | source)
XLA Modules:
  0.0 223.1 jit_solution(16000012736286348097)
XLA Ops:
  0.6 0.0 copy-start
  0.6 0.7 convert_bitcast_fusion
  1.4 0.1 copy.8
  1.5 0.0 copy-start.6
  1.5 2.2 bitcast_multiply_fusion
  3.7 34.7 %shard_map.77 = bf16[3,4,32,512]{3,2,1,0:T(8,128)(2,1)} custom-call(bf16[3,4,32,512]{3,2,1,0:T(8,128)(2,1)} %bitcast.120), custom_call_target="tpu_custom_call" | custom-call | tf_op jit(solution)/shard_map/pallas_call | solution.py:210
  38.5 1.7 fusion.16
  40.2 0.0 copy-done.6
  40.2 0.9 convolution_convert_fusion.3.x_ref
  41.1 11.9 %shard_map.78 = bf16[4,128,512]{2,1,0:T(8,128)(2,1)} custom-call(bf16[128,512]{1,0:T(8,128)(2,1)} %convolution_convert_fusion.3.x_ref), custom_call_target="tpu_custom_call" | custom-call | tf_op jit(solution)/shard_map/pallas_call | solution.py:78
  53.0 2.6 %fusion.17 = (bf16[4,128,512]{2,1,0:T(8,128)(2,1)}, f32[4,128,512]{2,1,0:T(8,128)}) fusion(bf16[4,128,512]{2,1,0:T(8,128)(2,1)} %shard_map.78, bf16[6,4,4,128,128]{4,3,2,1,0:T(8,128)(2,1)S(1)} %bitcast_multiply_fusion), kind=kOutput, calls=%fused_computation.41 | convolution fusion | flops 268697600 | bytes 2621440 | tf_op jit(solution)/shard_map/jznv,zvs->jns/dot_general | solution.py:324
  55.7 1.7 dynamic-slice_bitcast_fusion.2.own_ref
  57.3 15.3 %shard_map.79 = f32[128,512]{1,0:T(8,128)} custom-call(bf16[4,128,512]{2,1,0:T(8,128)(2,1)} %get-tuple-element.11.x_ref, f32[128,512]{1,0:T(8,128)} %dynamic-slice_bitcast_fusion.2.own_ref), custom_call_target="tpu_custom_call" | custom-call | tf_op jit(solution)/shard_map/pallas_call | solution.py:48
  72.7 2.0 convolution_convert_fusion.2
  74.7 10.0 %shard_map.80 = bf16[4,128,512]{2,1,0:T(8,128)(2,1)} custom-call(bf16[128,512]{1,0:T(8,128)(2,1)} %bitcast.111), custom_call_target="tpu_custom_call" | custom-call | tf_op jit(solution)/shard_map/pallas_call | solution.py:78
  84.7 1.5 convolution_bitcast_fusion.1
  86.2 0.0 copy-start.3
  86.2 0.0 copy-start.4
  86.2 2.3 %fusion.18 = (bf16[4,128,512]{2,1,0:T(8,128)(2,1)}, f32[4,128,512]{2,1,0:T(8,128)S(1)}) fusion(f32[4,128,512]{2,1,0:T(8,128)S(1)} %convolution_bitcast_fusion.1, bf16[4,128,512]{2,1,0:T(8,128)(2,1)} %shard_map.78, bf16[6,4,4,128,128]{4,3,2,1,0:T(8,128)(2,1)S(1)} %bitcast_multiply_fusion), kind=kOutput, calls=%fused_computation.42 | convolution fusion | flops 268959744 | bytes 3670016 | tf_op jit(solution)/shard_map/jznv,zvs->jns/dot_general | solution.py:324
  88.5 0.7 dynamic-slice_bitcast_fusion.1.own_ref
  89.2 17.0 %shard_map.81 = f32[128,512]{1,0:T(8,128)} custom-call(bf16[4,128,512]{2,1,0:T(8,128)(2,1)} %get-tuple-element.13.x_ref, f32[128,512]{1,0:T(8,128)} %dynamic-slice_bitcast_fusion.1.own_ref), custom_call_target="tpu_custom_call" | custom-call | tf_op jit(solution)/shard_map/pallas_call | solution.py:48
  106.2 1.4 convolution_convert_fusion.1
  107.6 0.0 copy-start.5
  107.7 0.0 copy-done.3
  107.7 0.0 copy-done.4
  107.7 0.8 pad_maximum_fusion.f_ref
  108.5 0.0 copy-done.5
  108.5 10.0 %shard_map.82 = bf16[4,128,512]{2,1,0:T(8,128)(2,1)} custom-call(bf16[128,512]{1,0:T(8,128)(2,1)} %bitcast.114), custom_call_target="tpu_custom_call" | custom-call | tf_op jit(solution)/shard_map/pallas_call | solution.py:78
  118.5 0.0 copy-start.1
  118.5 1.5 convolution_bitcast_fusion
  120.0 1.5 convolution_bitcast_fusion.3
  121.5 0.0 copy-done.1
  121.5 0.4 fusion.1.x_ref
  122.0 0.0 copy-start.2
  122.0 1.0 copy-done.2
  122.9 0.7 dynamic-slice_bitcast_fusion.own_ref
  123.7 25.5 %shard_map.83 = f32[128,512]{1,0:T(8,128)} custom-call(f32[4,128,512]{2,1,0:T(8,128)} %copy-done.2, f32[128,512]{1,0:T(8,128)} %dynamic-slice_bitcast_fusion.own_ref), custom_call_target="tpu_custom_call" | custom-call | tf_op jit(solution)/shard_map/pallas_call | solution.py:48
  149.2 1.7 reshape.68.x_ref
  150.9 44.1 %shard_map.84 = (f32[32,16,128]{2,1,0:T(8,128)}, bf16[3,4,32,512]{3,2,1,0:T(8,128)(2,1)}, bf16[1,4,32,512]{3,2,1,0:T(8,128)(2,1)}) custom-call(f32[32,16,128]{2,1,0:T(8,128)} %reshape.68.x_ref, bf16[3,4,32,512]{3,2,1,0:T(8,128)(2,1)} %pad_maximum_fusion.f_ref, bf16[1,4,32,512]{3,2,1,0:T(8,128)(2,1)} %bitcast.122), custom_call_target="tpu_custom_call" | custom-call | tf_op jit(solution)/shard_map/pallas_call | solution.py:265
  195.0 1.0 reshape.76
  195.9 1.0 sub.14
  197.0 0.0 copy-done
  197.0 1.1 convolution_convert_fusion
  198.1 21.7 %shard_map.85 = bf16[1,4,32,512]{3,2,1,0:T(8,128)(2,1)} custom-call(bf16[1,4,32,512]{3,2,1,0:T(8,128)(2,1)} %bitcast.115), custom_call_target="tpu_custom_call" | custom-call | tf_op jit(solution)/shard_map/pallas_call | solution.py:210
  219.8 1.8 copy.17
  221.6 1.6 copy.18
  (1 shorter events, 0.0 us)
Async XLA Ops:
  0.6 196.4 %copy-start = (f32[1,1,128,128]{3,2,1,0:T(8,128)S(1)}, f32[1,1,128,128]{3,2,1,0:T(8,128)}, u32[]{:S(2)}) copy-start(f32[1,1,128,128]{3,2,1,0:T(8,128)} %param.11) | copy-start | bytes 196612
  1.5 38.7 %copy-start.6 = (f32[1,3,1,1,128,128]{5,4,3,2,1,0:T(8,128)S(1)}, f32[1,3,1,1,128,128]{5,4,3,2,1,0:T(8,128)}, u32[]{:S(2)}) copy-start(f32[1,3,1,1,128,128]{5,4,3,2,1,0:T(8,128)} %param.10) | copy-start | bytes 589828
  86.2 21.5 %copy-start.3 = (bf16[128,512]{1,0:T(8,128)(2,1)S(1)}, bf16[128,512]{1,0:T(8,128)(2,1)}, u32[]{:S(2)}) copy-start(bf16[128,512]{1,0:T(8,128)(2,1)} %convolution_convert_fusion.3.x_ref) | copy-start | bytes 393220
  86.2 21.5 %copy-start.4 = (bf16[512,128]{0,1:T(8,128)(2,1)S(1)}, bf16[512,128]{0,1:T(8,128)(2,1)}, u32[]{:S(2)}) copy-start(bf16[512,128]{0,1:T(8,128)(2,1)} %convolution_convert_fusion.2) | copy-start | bytes 393220
  107.6 0.8 copy-start.5
  118.5 3.0 %copy-start.1 = (bf16[4,128,512]{2,1,0:T(8,128)(2,1)S(1)}, bf16[4,128,512]{2,1,0:T(8,128)(2,1)}, u32[]{:S(2)}) copy-start(bf16[4,128,512]{2,1,0:T(8,128)(2,1)} %shard_map.78) | copy-start | bytes 1572868
  122.0 1.0 copy-start.2

commit v5 on v4

--- a/solution.py
+++ b/solution.py
@@ -283,6 +283,102 @@
     )(chunks, forest, root_in)
 
 
+def forest_solve(local_forest, masked, inverses, cid):
+    levels, g, slice_rows, cols = local_forest.shape
+    rows = g * slice_rows
+    f32, bf16 = jnp.float32, jnp.bfloat16
+
+    def kernel(f_ref, w_ref, inv_ref, sol_ref, share_ref,
+               placed, gath, tot, sb, rrecv, rootrecv,
+               ps, pr, plsem, gs, gr, rs_s, rs_r):
+        p = lax.axis_index("prow")
+        q = lax.axis_index("pcol")
+        barrier = pltpu.get_barrier_semaphore()
+        _grid_barrier_signals(barrier, g, p, q)
+        pl.semaphore_wait(barrier, g * g - 1)
+        _permute_start(f_ref, placed, True, ps, pr, plsem)()
+        tot[...] = jnp.zeros(tot.shape, f32)
+        pending = []
+        for t in range(levels):
+            rhs = placed[t].reshape(rows, cols).astype(f32)
+            if t > 0:
+                for copy in pending:
+                    copy.wait()
+                red = tot[t - 1, q]
+                for d in range(g - 1):
+                    red = red + rrecv[t - 1, d].astype(f32)
+                rhs = rhs - red
+            ans = jnp.dot(inv_ref[t], rhs, precision=lax.Precision.HIGHEST,
+                          preferred_element_type=f32).astype(bf16)
+            sol_ref[t] = ans.reshape(g, slice_rows, cols)
+            gath[t, p] = ans
+            copies = []
+            for d in range(1, g):
+                copy = pltpu.make_async_remote_copy(
+                    gath.at[t, p], gath.at[t, p], gs.at[t, d - 1], gr.at[t, d - 1],
+                    device_id={"prow": (p + d) % g}, device_id_type=MESH)
+                copy.start()
+                copies.append(copy)
+            for copy in copies:
+                copy.wait()
+            for target in range(t + 1, levels + 1):
+                pair = pair_slot(t, target)
+
+                def body(j, carry, t=t, target=target, pair=pair):
+                    acc = tot[target - 1, j]
+                    for z in range(g):
+                        acc = acc + jnp.dot(w_ref[pair, j, z], gath[t, z],
+                                            preferred_element_type=f32)
+                    tot[target - 1, j] = acc
+                    return carry
+
+                lax.fori_loop(0, g, body, 0)
+            pending = []
+            if t + 1 < levels:
+                sb[t] = tot[t].astype(bf16)
+                src, dst = sb.at[t], rrecv.at[t]
+            else:
+                src, dst = tot.at[t], rootrecv
+            for d in range(1, g):
+                peer = (q + d) % g
+                copy = pltpu.make_async_remote_copy(
+                    src.at[peer], dst.at[d - 1], rs_s.at[t, d - 1], rs_r.at[t, d - 1],
+                    device_id={"pcol": peer}, device_id_type=MESH)
+                copy.start()
+                pending.append(copy)
+        for copy in pending:
+            copy.wait()
+        share = tot[levels - 1, q]
+        for d in range(g - 1):
+            share = share + rootrecv[d]
+        share_ref[...] = share
+
+    return pl.pallas_call(
+        kernel,
+        out_shape=(
+            jax.ShapeDtypeStruct(local_forest.shape, bf16),
+            jax.ShapeDtypeStruct((rows, cols), f32),
+        ),
+        in_specs=[VMEM_SPEC] * 3,
+        out_specs=(VMEM_SPEC,) * 2,
+        scratch_shapes=[
+            pltpu.VMEM(local_forest.shape, bf16),
+            pltpu.VMEM((levels, g, rows, cols), bf16),
+            pltpu.VMEM((levels, g, rows, cols), f32),
+            pltpu.VMEM((levels - 1, g, rows, cols), bf16),
+            pltpu.VMEM((levels - 1, g - 1, rows, cols), bf16),
+            pltpu.VMEM((g - 1, rows, cols), f32),
+        ] + _permute_scratch(g) + [
+            pltpu.SemaphoreType.DMA((levels, g - 1)),
+            pltpu.SemaphoreType.DMA((levels, g - 1)),
+            pltpu.SemaphoreType.DMA((levels, g - 1)),
+            pltpu.SemaphoreType.DMA((levels, g - 1)),
+        ],
+        compiler_params=pltpu.CompilerParams(
+            collective_id=cid, has_side_effects=True, vmem_limit_bytes=48 * 1024 * 1024),
+    )(local_forest, masked, inverses)
+
+
 def shards(subtree_right_hand, root_rhs, blocks, pattern, forest_inverse, root_inverse):
     grid_size = lax.axis_size("prow")
     n_layer = lax.axis_size("layer")
@@ -291,49 +387,14 @@
     slice_rows = super_rows // grid_size
     local_forest = subtree_right_hand.reshape(3, grid_size, slice_rows, rhs_cols)
     local_root = root_rhs.reshape(1, grid_size, slice_rows, rhs_cols)
-    placed = permute_rows(local_forest, True, 40)
-    placed = placed.reshape(3, super_rows, rhs_cols)
     block_mask = pattern.reshape(6, grid_size, grid_size).astype(jnp.bfloat16)
     masked = (
         blocks.reshape(6, grid_size, grid_size, super_rows, super_rows)
         * block_mask[..., None, None]
     )
     inverses = forest_inverse.reshape(3, super_rows, super_rows)
-    solved = []
-    empty_rows = jnp.zeros((grid_size, super_rows, rhs_cols), jnp.float32)
-    totals = (empty_rows, empty_rows, empty_rows, empty_rows)
-    for tier_index in range(3):
-        right_hand_side = placed[tier_index].astype(jnp.float32)
-        if tier_index > 0:
-            rows = totals[tier_index]
-            own_rows = rows[lax.axis_index("pcol")]
-            reduced = reduce_scatter(rows.astype(jnp.bfloat16), own_rows, "pcol", 10 + tier_index, jnp.bfloat16)
-            right_hand_side = right_hand_side - reduced
-        answer = jnp.dot(
-            inverses[tier_index],
-            right_hand_side,
-            precision=lax.Precision.HIGHEST,
-            preferred_element_type=jnp.float32,
-        ).astype(jnp.bfloat16)
-        solved.append(answer)
-        block_pieces = all_gather(answer, "prow", grid_size, 20 + tier_index)
-        updated_rows = []
-        for target in range(4):
-            if target > tier_index:
-                factor_weights = masked[pair_slot(tier_index, target)]
-                term = jnp.einsum(
-                    "jznv,zvs->jns",
-                    factor_weights,
-                    block_pieces,
-                    preferred_element_type=jnp.float32,
-                )
-                updated_rows.append(totals[target] + term)
-            else:
-                updated_rows.append(totals[target])
-        totals = tuple(updated_rows)
-    row_share = reduce_scatter(totals[3], totals[3][lax.axis_index("pcol")], "pcol", 13, jnp.float32)
+    forest_solved, row_share = forest_solve(local_forest, masked, inverses, 10)
     chunks = row_share.reshape(n_layer, -1, 128)
-    forest_solved = jnp.stack(solved).reshape(3, grid_size, slice_rows, rhs_cols)
     reduced_root, forest_back, root_placed = root_exchange(chunks, forest_solved, local_root, 30)
     reduced_root = reduced_root.reshape(super_rows, rhs_cols)
     root_side = root_placed.reshape(super_rows, rhs_cols).astype(jnp.float32) - reduced_root

time: 224 us -> 180 us (0.80)
  Pallas kernels: 190 us -> 166 us
  matrix products: 15.2 us -> 1.05 us
  local copies, waits for them, and re-layouts: 12 us -> 5.96 us
    pallas_call x2 -> x1, Pallas kernels: 56.5 us -> 19.5 us  [permute_rows(): pl.pallas_call(kernel, out_shape=jax.ShapeDtypeStruct(x.shape, x.dtype),...]
    dot_general x9 -> x0, matrix products: 14.2 us -> none  [the longest x6 9.85 us: shards(): jnp.einsum('jznv,zvs->jns', factor_weights, block_pieces, preferred_eleme...]
    pallas_call x6 -> x1, Pallas kernels: 89.8 us -> 96.2 us  [forest_solve(): pl.pallas_call(kernel, out_shape=(jax.ShapeDtypeStruct(local_forest.shape...]
    pallas_call x1, Pallas kernels: 44.1 us -> 50.2 us  [root_exchange(): pl.pallas_call(kernel, out_shape=(jax.ShapeDtypeStruct(chunks.shape, chun...]
    squeeze x3 -> x0, local copies, waits for them, and re-layouts: 3.12 us -> none  [the longest x2 2.39 us: shards(): own_rows = rows[lax.axis_index('pcol')]]
where the time goes in v5:
time: 180 us; the launch traced here: 178 us
  Pallas kernels  166 us (92%)
  local copies, waits for them, and re-layouts  5.96 us (3%)
  other arithmetic  3.94 us (2%)
    pallas_call x1, Pallas kernels, forest_solve(): pl.pallas_call(kernel, out_shape=(jax.ShapeDtypeStruct(local_forest.shape...  96.2 us
    pallas_call x1, Pallas kernels, root_exchange(): pl.pallas_call(kernel, out_shape=(jax.ShapeDtypeStruct(chunks.shape, chun...  50.2 us
    pallas_call x1, Pallas kernels, permute_rows(): pl.pallas_call(kernel, out_shape=jax.ShapeDtypeStruct(x.shape, x.dtype),...  19.5 us
    unnamed x10, local copies, waits for them, and re-layouts  4.09 us

profile of v5, /device:TPU:6, one launch (start us, length us, event | category | flops | bytes accessed | tf_op | source)
XLA Modules:
  0.0 177.6 jit_solution(9036239197714115046)
XLA Ops:
  0.6 0.0 copy-start
  0.6 0.7 convert_bitcast_fusion
  1.4 0.1 copy.8
  1.5 0.0 copy-start.1
  1.5 0.0 copy-start.3
  1.5 2.2 %bitcast_multiply_fusion.w_ref = bf16[6,4,4,128,128]{4,3,2,1,0:T(8,128)(2,1)S(1)} fusion(bf16[1,6,1,1,4,4,128,128]{7,6,5,4,3,2,1,0:T(8,128)(2,1)} %param.8, bf16[6,4,4]{2,1,0:T(4,128)(2,1)S(1)} %copy.8), kind=kLoop, calls=%fused_computation | loop fusion | flops 1572864 | bytes 6291648 | tf_op jit(solution)/shard_map/mul | solution.py:392
  3.7 0.0 copy-done.1
  3.7 0.0 copy-done.3
  3.8 96.2 %shard_map.77 = (bf16[3,4,32,512]{3,2,1,0:T(8,128)(2,1)S(1)}, f32[128,512]{1,0:T(8,128)S(1)}) custom-call(bf16[3,4,32,512]{3,2,1,0:T(8,128)(2,1)S(1)} %bitcast.18, bf16[6,4,4,128,128]{4,3,2,1,0:T(8,128)(2,1)S(1)} %bitcast_multiply_fusion.w_ref, f32[3,128,128]{2,1,0:T(8,128)S(1)} %bitcast.19), custom_call_target="tpu_custom_call" | custom-call | tf_op jit(solution)/shard_map/pallas_call | solution.py:356
  100.0 0.0 copy-start.2
  100.0 0.7 copy-done.2
  100.7 0.7 reshape.47.x_ref
  101.5 50.2 %shard_map.78 = (f32[32,16,128]{2,1,0:T(8,128)}, bf16[3,4,32,512]{3,2,1,0:T(8,128)(2,1)}, bf16[1,4,32,512]{3,2,1,0:T(8,128)(2,1)}) custom-call(f32[32,16,128]{2,1,0:T(8,128)} %reshape.47.x_ref, bf16[3,4,32,512]{3,2,1,0:T(8,128)(2,1)} %copy-done.2, bf16[1,4,32,512]{3,2,1,0:T(8,128)(2,1)} %bitcast.23), custom_call_target="tpu_custom_call" | custom-call | tf_op jit(solution)/shard_map/pallas_call | solution.py:265
  151.7 1.0 reshape.53
  152.7 1.0 sub.6
  153.7 0.0 copy-done
  153.7 1.1 convolution_convert_fusion
  154.8 19.5 %shard_map.79 = bf16[1,4,32,512]{3,2,1,0:T(8,128)(2,1)} custom-call(bf16[1,4,32,512]{3,2,1,0:T(8,128)(2,1)} %bitcast.20), custom_call_target="tpu_custom_call" | custom-call | tf_op jit(solution)/shard_map/pallas_call | solution.py:210
  174.3 1.8 copy.11
  176.1 1.6 copy.12
  (1 shorter events, 0.0 us)
Async XLA Ops:
  0.6 153.1 %copy-start = (f32[1,1,128,128]{3,2,1,0:T(8,128)S(1)}, f32[1,1,128,128]{3,2,1,0:T(8,128)}, u32[]{:S(2)}) copy-start(f32[1,1,128,128]{3,2,1,0:T(8,128)} %param.11) | copy-start | bytes 196612
  1.5 2.2 %copy-start.1 = (bf16[1,384,512]{2,1,0:T(8,128)(2,1)S(1)}, bf16[1,384,512]{2,1,0:T(8,128)(2,1)}, u32[]{:S(2)}) copy-start(bf16[1,384,512]{2,1,0:T(8,128)(2,1)} %param.6) | copy-start | bytes 1179652
  1.5 2.2 %copy-start.3 = (f32[1,3,1,1,128,128]{5,4,3,2,1,0:T(8,128)S(1)}, f32[1,3,1,1,128,128]{5,4,3,2,1,0:T(8,128)}, u32[]{:S(2)}) copy-start(f32[1,3,1,1,128,128]{5,4,3,2,1,0:T(8,128)} %param.10) | copy-start | bytes 589828
  100.0 0.7 copy-start.2

commit v6 on v5

--- a/solution.py
+++ b/solution.py
@@ -283,22 +283,39 @@
     )(chunks, forest, root_in)
 
 
-def forest_solve(local_forest, masked, inverses, cid):
+def solve_all(local_forest, local_root, masked, inverses, root_inverse, n_layer, cid):
     levels, g, slice_rows, cols = local_forest.shape
     rows = g * slice_rows
     f32, bf16 = jnp.float32, jnp.bfloat16
-
-    def kernel(f_ref, w_ref, inv_ref, sol_ref, share_ref,
-               placed, gath, tot, sb, rrecv, rootrecv,
-               ps, pr, plsem, gs, gr, rs_s, rs_r):
+    row_blocks = rows // 8
+    col_parts = n_layer // row_blocks
+    chunk_cols = cols // col_parts
+
+    def chunk(ref, c):
+        r0 = pl.multiple_of((c // col_parts) * 8, 8)
+        c0 = pl.multiple_of((c % col_parts) * chunk_cols, chunk_cols)
+        return ref.at[pl.ds(r0, 8), pl.ds(c0, chunk_cols)]
+
+    def kernel(f_ref, r_ref, w_ref, inv_ref, rinv_ref, fo_ref, ro_ref,
+               placed, placed_root, sol, root_sol, gath, tot, sb, rrecv, rootrecv,
+               share_buf, recv_layer, part, full,
+               gs, gr, rs_s, rs_r, ls, lr, hs, hr, *perm_sems):
         p = lax.axis_index("prow")
         q = lax.axis_index("pcol")
+        me = lax.axis_index("layer")
+        perm = [perm_sems[3 * i:3 * i + 3] for i in range(levels + 3)]
         barrier = pltpu.get_barrier_semaphore()
         _grid_barrier_signals(barrier, g, p, q)
-        pl.semaphore_wait(barrier, g * g - 1)
-        _permute_start(f_ref, placed, True, ps, pr, plsem)()
+        for d in range(1, n_layer):
+            pl.semaphore_signal(barrier, 1, device_id={"layer": (me + d) % n_layer},
+                                device_id_type=MESH)
+        pl.semaphore_wait(barrier, g * g - 1 + n_layer - 1)
+        forest_in = _permute_start(f_ref, placed, True, *perm[0])
+        root_in = _permute_start(r_ref, placed_root, True, *perm[1])
+        forest_in()
         tot[...] = jnp.zeros(tot.shape, f32)
         pending = []
+        outs = []
         for t in range(levels):
             rhs = placed[t].reshape(rows, cols).astype(f32)
             if t > 0:
@@ -310,7 +327,7 @@
                 rhs = rhs - red
             ans = jnp.dot(inv_ref[t], rhs, precision=lax.Precision.HIGHEST,
                           preferred_element_type=f32).astype(bf16)
-            sol_ref[t] = ans.reshape(g, slice_rows, cols)
+            sol[t] = ans.reshape(g, slice_rows, cols)
             gath[t, p] = ans
             copies = []
             for d in range(1, g):
@@ -319,6 +336,8 @@
                     device_id={"prow": (p + d) % g}, device_id_type=MESH)
                 copy.start()
                 copies.append(copy)
+            outs.append(_permute_start(sol.at[pl.ds(t, 1)], fo_ref.at[pl.ds(t, 1)], False,
+                                       *perm[3 + t]))
             for copy in copies:
                 copy.wait()
             for target in range(t + 1, levels + 1):
@@ -351,32 +370,78 @@
         share = tot[levels - 1, q]
         for d in range(g - 1):
             share = share + rootrecv[d]
-        share_ref[...] = share
+        share_buf[...] = share
+        copies = []
+        for d in range(1, n_layer):
+            peer = (me + d) % n_layer
+            copy = pltpu.make_async_remote_copy(
+                chunk(share_buf, peer), recv_layer.at[d - 1], ls.at[d - 1], lr.at[d - 1],
+                device_id={"layer": peer}, device_id_type=MESH)
+            copy.start()
+            copies.append(copy)
+        for copy in copies:
+            copy.wait()
+        r0 = pl.multiple_of((me // col_parts) * 8, 8)
+        c0 = pl.multiple_of((me % col_parts) * chunk_cols, chunk_cols)
+        total = share_buf[pl.ds(r0, 8), pl.ds(c0, chunk_cols)]
+        for d in range(n_layer - 1):
+            total = total + recv_layer[d]
+        part[...] = total
+        full[pl.ds(r0, 8), pl.ds(c0, chunk_cols)] = total
+        copies = []
+        for d in range(1, n_layer):
+            peer = (me + d) % n_layer
+            copy = pltpu.make_async_remote_copy(
+                part, chunk(full, me), hs.at[d - 1], hr.at[d - 1],
+                device_id={"layer": peer}, device_id_type=MESH)
+            copy.start()
+            copies.append(copy)
+        for copy in copies:
+            copy.wait()
+        root_in()
+        side = placed_root[0].reshape(rows, cols).astype(f32) - full[...]
+        answer = jnp.dot(rinv_ref[...], side, precision=lax.Precision.HIGHEST,
+                         preferred_element_type=f32).astype(bf16)
+        root_sol[0] = answer.reshape(g, slice_rows, cols)
+        root_out = _permute_start(root_sol, ro_ref, False, *perm[2])
+        for wait in outs:
+            wait()
+        root_out()
 
     return pl.pallas_call(
         kernel,
         out_shape=(
             jax.ShapeDtypeStruct(local_forest.shape, bf16),
-            jax.ShapeDtypeStruct((rows, cols), f32),
+            jax.ShapeDtypeStruct(local_root.shape, bf16),
         ),
-        in_specs=[VMEM_SPEC] * 3,
+        in_specs=[VMEM_SPEC] * 5,
         out_specs=(VMEM_SPEC,) * 2,
         scratch_shapes=[
             pltpu.VMEM(local_forest.shape, bf16),
+            pltpu.VMEM(local_root.shape, bf16),
+            pltpu.VMEM(local_forest.shape, bf16),
+            pltpu.VMEM(local_root.shape, bf16),
             pltpu.VMEM((levels, g, rows, cols), bf16),
             pltpu.VMEM((levels, g, rows, cols), f32),
             pltpu.VMEM((levels - 1, g, rows, cols), bf16),
             pltpu.VMEM((levels - 1, g - 1, rows, cols), bf16),
             pltpu.VMEM((g - 1, rows, cols), f32),
-        ] + _permute_scratch(g) + [
+            pltpu.VMEM((rows, cols), f32),
+            pltpu.VMEM((n_layer - 1, 8, chunk_cols), f32),
+            pltpu.VMEM((8, chunk_cols), f32),
+            pltpu.VMEM((rows, cols), f32),
             pltpu.SemaphoreType.DMA((levels, g - 1)),
             pltpu.SemaphoreType.DMA((levels, g - 1)),
             pltpu.SemaphoreType.DMA((levels, g - 1)),
             pltpu.SemaphoreType.DMA((levels, g - 1)),
-        ],
+            pltpu.SemaphoreType.DMA((n_layer - 1,)),
+            pltpu.SemaphoreType.DMA((n_layer - 1,)),
+            pltpu.SemaphoreType.DMA((n_layer - 1,)),
+            pltpu.SemaphoreType.DMA((n_layer - 1,)),
+        ] + _permute_scratch(g) * (levels + 3),
         compiler_params=pltpu.CompilerParams(
             collective_id=cid, has_side_effects=True, vmem_limit_bytes=48 * 1024 * 1024),
-    )(local_forest, masked, inverses)
+    )(local_forest, local_root, masked, inverses, root_inverse)
 
 
 def shards(subtree_right_hand, root_rhs, blocks, pattern, forest_inverse, root_inverse):
@@ -393,18 +458,9 @@
         * block_mask[..., None, None]
     )
     inverses = forest_inverse.reshape(3, super_rows, super_rows)
-    forest_solved, row_share = forest_solve(local_forest, masked, inverses, 10)
-    chunks = row_share.reshape(n_layer, -1, 128)
-    reduced_root, forest_back, root_placed = root_exchange(chunks, forest_solved, local_root, 30)
-    reduced_root = reduced_root.reshape(super_rows, rhs_cols)
-    root_side = root_placed.reshape(super_rows, rhs_cols).astype(jnp.float32) - reduced_root
-    root_answer = jnp.dot(
-        root_inverse.reshape(super_rows, super_rows),
-        root_side,
-        precision=lax.Precision.HIGHEST,
-        preferred_element_type=jnp.float32,
-    ).astype(jnp.bfloat16)
-    root_back = permute_rows(root_answer.reshape(1, grid_size, slice_rows, rhs_cols), False, 41)
+    forest_back, root_back = solve_all(
+        local_forest, local_root, masked, inverses,
+        root_inverse.reshape(super_rows, super_rows), n_layer, 10)
     forest_out = forest_back.reshape(1, 3 * super_rows, rhs_cols)
     root_out = root_back.reshape(super_rows, rhs_cols)
     return (forest_out, root_out)

time: 180 us -> 167 us (0.928)
  Pallas kernels: 166 us -> 161 us
  local copies, waits for them, and re-layouts: 5.96 us -> 1.54 us
    pallas_call x3 -> x1, Pallas kernels: 166 us -> 161 us  [solve_all(): pl.pallas_call(kernel, out_shape=(jax.ShapeDtypeStruct(local_forest.shape...]
    unnamed x10, local copies, waits for them, and re-layouts: 4.09 us -> 1.42 us
where the time goes in v6:
time: 167 us; the launch traced here: 166 us
  Pallas kernels  161 us (96%)
  other arithmetic  2.93 us (2%)
    pallas_call x1, Pallas kernels, solve_all(): pl.pallas_call(kernel, out_shape=(jax.ShapeDtypeStruct(local_forest.shape...  161 us

profile of v6, /device:TPU:6, one launch (start us, length us, event | category | flops | bytes accessed | tf_op | source)
XLA Modules:
  0.0 166.4 jit_solution(16434219570395730376)
XLA Ops:
  0.6 0.7 convert_bitcast_fusion
  1.3 0.1 copy.8
  1.5 0.0 copy-start
  1.5 0.0 copy-start.1
  1.5 0.0 copy-start.2
  1.5 0.0 copy-start.3
  1.5 2.2 %bitcast_multiply_fusion.w_ref = bf16[6,4,4,128,128]{4,3,2,1,0:T(8,128)(2,1)S(1)} fusion(bf16[1,6,1,1,4,4,128,128]{7,6,5,4,3,2,1,0:T(8,128)(2,1)} %param.8, bf16[6,4,4]{2,1,0:T(4,128)(2,1)S(1)} %copy.8), kind=kLoop, calls=%fused_computation | loop fusion | flops 1572864 | bytes 6291648 | tf_op jit(solution)/shard_map/mul | solution.py:457
  3.7 0.0 copy-done
  3.7 0.0 copy-done.1
  3.7 0.0 copy-done.2
  3.7 0.0 copy-done.3
  3.8 161.2 %shard_map.77 = (bf16[3,4,32,512]{3,2,1,0:T(8,128)(2,1)S(1)}, bf16[1,4,32,512]{3,2,1,0:T(8,128)(2,1)S(1)}) custom-call(bf16[3,4,32,512]{3,2,1,0:T(8,128)(2,1)S(1)} %bitcast.11, bf16[1,4,32,512]{3,2,1,0:T(8,128)(2,1)S(1)} %bitcast.13, bf16[6,4,4,128,128]{4,3,2,1,0:T(8,128)(2,1)S(1)} %bitcast_multiply_fusion.w_ref, f32[3,128,128]{2,1,0:T(8,128)S(1)} %bitcast.12, ...), custom_call_target="tpu_custom_call" | custom-call | tf_op jit(solution)/shard_map/pallas_call | solution.py:411
  164.9 0.7 copy.11
  165.7 0.7 copy.12
Async XLA Ops:
  1.5 2.3 %copy-start = (bf16[1,384,512]{2,1,0:T(8,128)(2,1)S(1)}, bf16[1,384,512]{2,1,0:T(8,128)(2,1)}, u32[]{:S(2)}) copy-start(bf16[1,384,512]{2,1,0:T(8,128)(2,1)} %param.6) | copy-start | bytes 1179652
  1.5 2.3 %copy-start.1 = (f32[1,3,1,1,128,128]{5,4,3,2,1,0:T(8,128)S(1)}, f32[1,3,1,1,128,128]{5,4,3,2,1,0:T(8,128)}, u32[]{:S(2)}) copy-start(f32[1,3,1,1,128,128]{5,4,3,2,1,0:T(8,128)} %param.10) | copy-start | bytes 589828
  1.5 2.3 %copy-start.2 = (bf16[128,512]{1,0:T(8,128)(2,1)S(1)}, bf16[128,512]{1,0:T(8,128)(2,1)}, u32[]{:S(2)}) copy-start(bf16[128,512]{1,0:T(8,128)(2,1)} %param.7) | copy-start | bytes 393220
  1.5 2.3 %copy-start.3 = (f32[1,1,128,128]{3,2,1,0:T(8,128)S(1)}, f32[1,1,128,128]{3,2,1,0:T(8,128)}, u32[]{:S(2)}) copy-start(f32[1,1,128,128]{3,2,1,0:T(8,128)} %param.11) | copy-start | bytes 196612

commit v7 on v6

--- a/solution.py
+++ b/solution.py
@@ -283,7 +283,7 @@
     )(chunks, forest, root_in)
 
 
-def solve_all(local_forest, local_root, masked, inverses, root_inverse, n_layer, cid):
+def solve_all(local_forest, local_root, factors, pattern, inverses, root_inverse, n_layer, cid):
     levels, g, slice_rows, cols = local_forest.shape
     rows = g * slice_rows
     f32, bf16 = jnp.float32, jnp.bfloat16
@@ -296,7 +296,7 @@
         c0 = pl.multiple_of((c % col_parts) * chunk_cols, chunk_cols)
         return ref.at[pl.ds(r0, 8), pl.ds(c0, chunk_cols)]
 
-    def kernel(f_ref, r_ref, w_ref, inv_ref, rinv_ref, fo_ref, ro_ref,
+    def kernel(f_ref, r_ref, w_ref, pat_ref, inv_ref, rinv_ref, fo_ref, ro_ref,
                placed, placed_root, sol, root_sol, gath, tot, sb, rrecv, rootrecv,
                share_buf, recv_layer, part, full,
                gs, gr, rs_s, rs_r, ls, lr, hs, hr, *perm_sems):
@@ -312,8 +312,8 @@
         pl.semaphore_wait(barrier, g * g - 1 + n_layer - 1)
         forest_in = _permute_start(f_ref, placed, True, *perm[0])
         root_in = _permute_start(r_ref, placed_root, True, *perm[1])
+        tot[...] = jnp.zeros(tot.shape, f32)
         forest_in()
-        tot[...] = jnp.zeros(tot.shape, f32)
         pending = []
         outs = []
         for t in range(levels):
@@ -346,7 +346,8 @@
                 def body(j, carry, t=t, target=target, pair=pair):
                     acc = tot[target - 1, j]
                     for z in range(g):
-                        acc = acc + jnp.dot(w_ref[pair, j, z], gath[t, z],
+                        present = pat_ref[pair, j, z].astype(f32).astype(bf16)
+                        acc = acc + jnp.dot(w_ref[pair, j, z] * present, gath[t, z],
                                             preferred_element_type=f32)
                     tot[target - 1, j] = acc
                     return carry
@@ -414,7 +415,8 @@
             jax.ShapeDtypeStruct(local_forest.shape, bf16),
             jax.ShapeDtypeStruct(local_root.shape, bf16),
         ),
-        in_specs=[VMEM_SPEC] * 5,
+        in_specs=[VMEM_SPEC, VMEM_SPEC, VMEM_SPEC,
+                  pl.BlockSpec(memory_space=pltpu.SMEM), VMEM_SPEC, VMEM_SPEC],
         out_specs=(VMEM_SPEC,) * 2,
         scratch_shapes=[
             pltpu.VMEM(local_forest.shape, bf16),
@@ -441,7 +443,7 @@
         ] + _permute_scratch(g) * (levels + 3),
         compiler_params=pltpu.CompilerParams(
             collective_id=cid, has_side_effects=True, vmem_limit_bytes=48 * 1024 * 1024),
-    )(local_forest, local_root, masked, inverses, root_inverse)
+    )(local_forest, local_root, factors, pattern, inverses, root_inverse)
 
 
 def shards(subtree_right_hand, root_rhs, blocks, pattern, forest_inverse, root_inverse):
@@ -452,14 +454,11 @@
     slice_rows = super_rows // grid_size
     local_forest = subtree_right_hand.reshape(3, grid_size, slice_rows, rhs_cols)
     local_root = root_rhs.reshape(1, grid_size, slice_rows, rhs_cols)
-    block_mask = pattern.reshape(6, grid_size, grid_size).astype(jnp.bfloat16)
-    masked = (
-        blocks.reshape(6, grid_size, grid_size, super_rows, super_rows)
-        * block_mask[..., None, None]
-    )
+    factors = blocks.reshape(6, grid_size, grid_size, super_rows, super_rows)
+    present = pattern.reshape(6, grid_size, grid_size)
     inverses = forest_inverse.reshape(3, super_rows, super_rows)
     forest_back, root_back = solve_all(
-        local_forest, local_root, masked, inverses,
+        local_forest, local_root, factors, present, inverses,
         root_inverse.reshape(super_rows, super_rows), n_layer, 10)
     forest_out = forest_back.reshape(1, 3 * super_rows, rhs_cols)
     root_out = root_back.reshape(super_rows, rhs_cols)

time: 167 us -> 170 us (1.018); the launches traced: 166 us -> 168 us
  local copies, waits for them, and re-layouts: 1.54 us -> 7.76 us
  other arithmetic: 2.93 us -> 0 us
  Pallas kernels: 161 us -> 159 us
    unnamed x10 -> x12, local copies, waits for them, and re-layouts: 1.42 us -> 6.96 us
    mul x1 -> x0, other arithmetic: 2.23 us -> none  [shards(): blocks.reshape(6, grid_size, grid_size, super_rows, super_rows)]
    pallas_call x1, Pallas kernels: 161 us -> 159 us  [solve_all(): pl.pallas_call(kernel, out_shape=(jax.ShapeDtypeStruct(local_forest.shape...]
where the time goes in v7:
time: 170 us; the launch traced here: 168 us
  Pallas kernels  159 us (94%)
  local copies, waits for them, and re-layouts  7.76 us (5%)
    pallas_call x1, Pallas kernels, solve_all(): pl.pallas_call(kernel, out_shape=(jax.ShapeDtypeStruct(local_forest.shape...  159 us
    unnamed x12, local copies, waits for them, and re-layouts  6.96 us

profile of v7, /device:TPU:6, one launch (start us, length us, event | category | flops | bytes accessed | tf_op | source)
XLA Modules:
  0.0 167.6 jit_solution(7568989210055292426)
XLA Ops:
  0.6 0.8 copy.8.pat_ref
  1.4 0.0 copy-start
  1.4 1.9 %copy-done = bf16[1,6,1,1,4,4,128,128]{7,6,5,4,3,2,1,0:T(8,128)(2,1)S(1)} copy-done((bf16[1,6,1,1,4,4,128,128]{7,6,5,4,3,2,1,0:T(8,128)(2,1)S(1)}, bf16[1,6,1,1,4,4,128,128]{7,6,5,4,3,2,1,0:T(8,128)(2,1)}, u32[]{:S(2)}) %copy-start) | copy-done | bytes 3145752
  3.3 0.0 copy-start.1
  3.3 1.0 copy-done.1
  4.3 0.0 copy-start.2
  4.3 0.9 copy-done.2
  5.2 0.0 copy-start.3
  5.2 0.9 copy-done.3
  6.1 0.0 copy-start.4
  6.2 0.8 copy-done.4
  7.0 159.2 %shard_map.77 = (bf16[3,4,32,512]{3,2,1,0:T(8,128)(2,1)S(1)}, bf16[1,4,32,512]{3,2,1,0:T(8,128)(2,1)S(1)}) custom-call(bf16[3,4,32,512]{3,2,1,0:T(8,128)(2,1)S(1)} %bitcast.9, bf16[1,4,32,512]{3,2,1,0:T(8,128)(2,1)S(1)} %bitcast.12, bf16[6,4,4,128,128]{4,3,2,1,0:T(8,128)(2,1)S(1)} %bitcast.8, s32[6,4,4]{2,1,0:T(4,128)S(1)} %copy.8.pat_ref, ...), custom_call_target="tpu_custom_call" | custom-call | tf_op jit(solution)/shard_map/pallas_call | solution.py:412
  166.2 0.7 copy.11
  167.0 0.7 copy.12
Async XLA Ops:
  1.4 1.9 %copy-start = (bf16[1,6,1,1,4,4,128,128]{7,6,5,4,3,2,1,0:T(8,128)(2,1)S(1)}, bf16[1,6,1,1,4,4,128,128]{7,6,5,4,3,2,1,0:T(8,128)(2,1)}, u32[]{:S(2)}) copy-start(bf16[1,6,1,1,4,4,128,128]{7,6,5,4,3,2,1,0:T(8,128)(2,1)} %param.8) | copy-start | bytes 9437188
  3.3 1.0 copy-start.1
  4.3 0.9 copy-start.2
  5.2 0.9 copy-start.3
  6.1 0.8 copy-start.4

commit v8 on v7

--- a/solution.py
+++ b/solution.py
@@ -7,6 +7,7 @@
 
 MESH = pl.DeviceIdType.MESH
 VMEM_SPEC = pl.BlockSpec(memory_space=pltpu.VMEM)
+ANY_SPEC = pl.BlockSpec(memory_space=pl.ANY)
 
 
 def pair_slot(source, target):
@@ -296,14 +297,18 @@
         c0 = pl.multiple_of((c % col_parts) * chunk_cols, chunk_cols)
         return ref.at[pl.ds(r0, 8), pl.ds(c0, chunk_cols)]
 
-    def kernel(f_ref, r_ref, w_ref, pat_ref, inv_ref, rinv_ref, fo_ref, ro_ref,
+    def kernel(f_ref, r_ref, w_hbm, pat_ref, inv_hbm, rinv_hbm, fo_ref, ro_ref,
                placed, placed_root, sol, root_sol, gath, tot, sb, rrecv, rootrecv,
-               share_buf, recv_layer, part, full,
+               share_buf, recv_layer, part, full, w_ref, inv_ref, rinv_ref, load_sems,
                gs, gr, rs_s, rs_r, ls, lr, hs, hr, *perm_sems):
         p = lax.axis_index("prow")
         q = lax.axis_index("pcol")
         me = lax.axis_index("layer")
         perm = [perm_sems[3 * i:3 * i + 3] for i in range(levels + 3)]
+        loads = [pltpu.make_async_copy(src, dst, load_sems.at[i]) for i, (src, dst) in
+                 enumerate(((inv_hbm, inv_ref), (w_hbm, w_ref), (rinv_hbm, rinv_ref)))]
+        for load in loads:
+            load.start()
         barrier = pltpu.get_barrier_semaphore()
         _grid_barrier_signals(barrier, g, p, q)
         for d in range(1, n_layer):
@@ -316,6 +321,7 @@
         forest_in()
         pending = []
         outs = []
+        loads[0].wait()
         for t in range(levels):
             rhs = placed[t].reshape(rows, cols).astype(f32)
             if t > 0:
@@ -340,6 +346,8 @@
                                        *perm[3 + t]))
             for copy in copies:
                 copy.wait()
+            if t == 0:
+                loads[1].wait()
             for target in range(t + 1, levels + 1):
                 pair = pair_slot(t, target)
 
@@ -400,6 +408,7 @@
         for copy in copies:
             copy.wait()
         root_in()
+        loads[2].wait()
         side = placed_root[0].reshape(rows, cols).astype(f32) - full[...]
         answer = jnp.dot(rinv_ref[...], side, precision=lax.Precision.HIGHEST,
                          preferred_element_type=f32).astype(bf16)
@@ -415,8 +424,8 @@
             jax.ShapeDtypeStruct(local_forest.shape, bf16),
             jax.ShapeDtypeStruct(local_root.shape, bf16),
         ),
-        in_specs=[VMEM_SPEC, VMEM_SPEC, VMEM_SPEC,
-                  pl.BlockSpec(memory_space=pltpu.SMEM), VMEM_SPEC, VMEM_SPEC],
+        in_specs=[ANY_SPEC, ANY_SPEC, ANY_SPEC,
+                  pl.BlockSpec(memory_space=pltpu.SMEM), ANY_SPEC, ANY_SPEC],
         out_specs=(VMEM_SPEC,) * 2,
         scratch_shapes=[
             pltpu.VMEM(local_forest.shape, bf16),
@@ -432,6 +441,10 @@
             pltpu.VMEM((n_layer - 1, 8, chunk_cols), f32),
             pltpu.VMEM((8, chunk_cols), f32),
             pltpu.VMEM((rows, cols), f32),
+            pltpu.VMEM(factors.shape, factors.dtype),
+            pltpu.VMEM(inverses.shape, f32),
+            pltpu.VMEM(root_inverse.shape, f32),
+            pltpu.SemaphoreType.DMA((3,)),
             pltpu.SemaphoreType.DMA((levels, g - 1)),
             pltpu.SemaphoreType.DMA((levels, g - 1)),
             pltpu.SemaphoreType.DMA((levels, g - 1)),
@@ -441,8 +454,7 @@
             pltpu.SemaphoreType.DMA((n_layer - 1,)),
             pltpu.SemaphoreType.DMA((n_layer - 1,)),
         ] + _permute_scratch(g) * (levels + 3),
-        compiler_params=pltpu.CompilerParams(
-            collective_id=cid, has_side_effects=True, vmem_limit_bytes=48 * 1024 * 1024),
+        compiler_params=_params(cid),
     )(local_forest, local_root, factors, pattern, inverses, root_inverse)
 
 

time: 170 us -> 169 us (level)
  local copies, waits for them, and re-layouts: 7.76 us -> 4.73 us
  Pallas kernels: 159 us -> 161 us
    unnamed x12 -> x2, local copies, waits for them, and re-layouts: 6.96 us -> 3.33 us
where the time goes in v8:
time: 169 us; the launch traced here: 166 us
  Pallas kernels  161 us (95%)
  local copies, waits for them, and re-layouts  4.73 us (3%)
    pallas_call x1, Pallas kernels, solve_all(): pl.pallas_call(kernel, out_shape=(jax.ShapeDtypeStruct(local_forest.shape...  161 us

profile of v8, /device:TPU:6, one launch (start us, length us, event | category | flops | bytes accessed | tf_op | source)
XLA Modules:
  0.0 166.0 jit_solution(3821076541838734347)
XLA Ops:
  0.6 1.4 copy.8.pat_ref
  2.0 160.6 %shard_map.77 = (bf16[3,4,32,512]{3,2,1,0:T(8,128)(2,1)}, bf16[1,4,32,512]{3,2,1,0:T(8,128)(2,1)}) custom-call(bf16[3,4,32,512]{3,2,1,0:T(8,128)(2,1)} %bitcast.9, bf16[1,4,32,512]{3,2,1,0:T(8,128)(2,1)} %bitcast.12, bf16[6,4,4,128,128]{4,3,2,1,0:T(8,128)(2,1)} %bitcast.8, s32[6,4,4]{2,1,0:T(4,128)} %copy.8.pat_ref, f32[3,128,128]{2,1,0:T(8,128)} %bitcast.11, ...), custom_call_target="tpu_custom_call" | custom-call | tf_op jit(solution)/shard_map/pallas_call | solution.py:421
  162.6 1.8 %copy.11 = bf16[1,384,512]{2,1,0:T(8,128)(2,1)} copy(bf16[1,384,512]{2,1,0:T(8,128)(2,1)} %bitcast.10) | data formatting | bytes 786432
  164.4 1.6 copy.12

commit v9 on v8

--- a/solution.py
+++ b/solution.py
@@ -288,19 +288,10 @@
     levels, g, slice_rows, cols = local_forest.shape
     rows = g * slice_rows
     f32, bf16 = jnp.float32, jnp.bfloat16
-    row_blocks = rows // 8
-    col_parts = n_layer // row_blocks
-    chunk_cols = cols // col_parts
-
-    def chunk(ref, c):
-        r0 = pl.multiple_of((c // col_parts) * 8, 8)
-        c0 = pl.multiple_of((c % col_parts) * chunk_cols, chunk_cols)
-        return ref.at[pl.ds(r0, 8), pl.ds(c0, chunk_cols)]
-
     def kernel(f_ref, r_ref, w_hbm, pat_ref, inv_hbm, rinv_hbm, fo_ref, ro_ref,
-               placed, placed_root, sol, root_sol, gath, tot, sb, rrecv, rootrecv,
-               share_buf, recv_layer, part, full, w_ref, inv_ref, rinv_ref, load_sems,
-               gs, gr, rs_s, rs_r, ls, lr, hs, hr, *perm_sems):
+               placed, placed_root, sol, root_sol, gath, tot, sb, rrecv,
+               recv_a, sbuf, recv_b, tbuf, recv_1, part, full, w_ref, inv_ref, rinv_ref, load_sems,
+               gs, gr, rs_s, rs_r, a_sem, b_send, b_recv, c1_send, c1_recv, hs, hr, *perm_sems):
         p = lax.axis_index("prow")
         q = lax.axis_index("pcol")
         me = lax.axis_index("layer")
@@ -361,52 +352,86 @@
                     return carry
 
                 lax.fori_loop(0, g, body, 0)
-            pending = []
             if t + 1 < levels:
+                pending = []
                 sb[t] = tot[t].astype(bf16)
-                src, dst = sb.at[t], rrecv.at[t]
+                for d in range(1, g):
+                    peer = (q + d) % g
+                    copy = pltpu.make_async_remote_copy(
+                        sb.at[t, peer], rrecv.at[t, d - 1], rs_s.at[t, d - 1], rs_r.at[t, d - 1],
+                        device_id={"pcol": peer}, device_id_type=MESH)
+                    copy.start()
+                    pending.append(copy)
+        core = me % 2
+        half = g // 2
+        copy = pltpu.make_async_remote_copy(
+            tot.at[levels - 1, pl.ds((1 - core) * half, half)], recv_a, a_sem.at[0], a_sem.at[1],
+            device_id={"layer": me + 1 - 2 * core}, device_id_type=MESH)
+        copy.start()
+        copy.wait()
+        sbuf[...] = tot[levels - 1, pl.ds(core * half, half)] + recv_a[...]
+        holder = q // half == core
+        for k in range(half):
+            j = core * half + k
+            off = (j - q + g) % g
+            copy = pltpu.make_async_remote_copy(
+                sbuf.at[k], recv_b.at[off], b_send.at[k], b_recv.at[off],
+                device_id={"pcol": j}, device_id_type=MESH)
+
+            @pl.when(j != q)
+            def _(copy=copy):
+                copy.start()
+                copy.wait_send()
+
+        n_h = n_layer // 2
+        m = me // 2
+        c_rows = rows // n_h
+        mine = pl.ds(pl.multiple_of(m * c_rows, 8), c_rows)
+
+        @pl.when(holder)
+        def _():
+            for off in range(1, g):
+                pltpu.make_async_copy(sbuf.at[0], recv_b.at[off], b_recv.at[off]).wait()
+            t_sum = sbuf[q - core * half]
+            for off in range(1, g):
+                t_sum = t_sum + recv_b[off]
+            tbuf[...] = t_sum
+            copies = []
+            for dm in range(1, n_h):
+                pm = (m + dm) % n_h
+                copy = pltpu.make_async_remote_copy(
+                    tbuf.at[pl.ds(pl.multiple_of(pm * c_rows, 8), c_rows)], recv_1.at[dm - 1],
+                    c1_send.at[dm - 1], c1_recv.at[dm - 1],
+                    device_id={"layer": 2 * pm + core}, device_id_type=MESH)
+                copy.start()
+                copies.append(copy)
+            for copy in copies:
+                copy.wait()
+            total = tbuf[mine]
+            for dm in range(n_h - 1):
+                total = total + recv_1[dm]
+            part[...] = total
+            full[mine] = total
+            copies = []
+            for d in range(1, n_layer):
+                copy = pltpu.make_async_remote_copy(
+                    part, full.at[mine], hs.at[d - 1], hr.at[m],
+                    device_id={"layer": (me + d) % n_layer}, device_id_type=MESH)
+                copy.start()
+                copies.append(copy)
+            for copy in copies:
+                copy.wait_send()
+
+        for dm in range(n_h):
+            mm = (m + dm) % n_h
+            arrival = pltpu.make_async_copy(
+                part, full.at[pl.ds(pl.multiple_of(mm * c_rows, 8), c_rows)], hr.at[mm])
+            if dm == 0:
+                @pl.when(jnp.logical_not(holder))
+                def _():
+                    arrival.wait()
             else:
-                src, dst = tot.at[t], rootrecv
-            for d in range(1, g):
-                peer = (q + d) % g
-                copy = pltpu.make_async_remote_copy(
-                    src.at[peer], dst.at[d - 1], rs_s.at[t, d - 1], rs_r.at[t, d - 1],
-                    device_id={"pcol": peer}, device_id_type=MESH)
-                copy.start()
-                pending.append(copy)
-        for copy in pending:
-            copy.wait()
-        share = tot[levels - 1, q]
-        for d in range(g - 1):
-            share = share + rootrecv[d]
-        share_buf[...] = share
-        copies = []
-        for d in range(1, n_layer):
-            peer = (me + d) % n_layer
-            copy = pltpu.make_async_remote_copy(
-                chunk(share_buf, peer), recv_layer.at[d - 1], ls.at[d - 1], lr.at[d - 1],
-                device_id={"layer": peer}, device_id_type=MESH)
-            copy.start()
-            copies.append(copy)
-        for copy in copies:
-            copy.wait()
-        r0 = pl.multiple_of((me // col_parts) * 8, 8)
-        c0 = pl.multiple_of((me % col_parts) * chunk_cols, chunk_cols)
-        total = share_buf[pl.ds(r0, 8), pl.ds(c0, chunk_cols)]
-        for d in range(n_layer - 1):
-            total = total + recv_layer[d]
-        part[...] = total
-        full[pl.ds(r0, 8), pl.ds(c0, chunk_cols)] = total
-        copies = []
-        for d in range(1, n_layer):
-            peer = (me + d) % n_layer
-            copy = pltpu.make_async_remote_copy(
-                part, chunk(full, me), hs.at[d - 1], hr.at[d - 1],
-                device_id={"layer": peer}, device_id_type=MESH)
-            copy.start()
-            copies.append(copy)
-        for copy in copies:
-            copy.wait()
+                arrival.wait()
         root_in()
         loads[2].wait()
         side = placed_root[0].reshape(rows, cols).astype(f32) - full[...]
@@ -436,10 +461,12 @@
             pltpu.VMEM((levels, g, rows, cols), f32),
             pltpu.VMEM((levels - 1, g, rows, cols), bf16),
             pltpu.VMEM((levels - 1, g - 1, rows, cols), bf16),
-            pltpu.VMEM((g - 1, rows, cols), f32),
+            pltpu.VMEM((g // 2, rows, cols), f32),
+            pltpu.VMEM((g // 2, rows, cols), f32),
+            pltpu.VMEM((g, rows, cols), f32),
             pltpu.VMEM((rows, cols), f32),
-            pltpu.VMEM((n_layer - 1, 8, chunk_cols), f32),
-            pltpu.VMEM((8, chunk_cols), f32),
+            pltpu.VMEM((max(n_layer // 2 - 1, 1), rows // (n_layer // 2), cols), f32),
+            pltpu.VMEM((rows // (n_layer // 2), cols), f32),
             pltpu.VMEM((rows, cols), f32),
             pltpu.VMEM(factors.shape, factors.dtype),
             pltpu.VMEM(inverses.shape, f32),
@@ -449,10 +476,13 @@
             pltpu.SemaphoreType.DMA((levels, g - 1)),
             pltpu.SemaphoreType.DMA((levels, g - 1)),
             pltpu.SemaphoreType.DMA((levels, g - 1)),
+            pltpu.SemaphoreType.DMA((2,)),
+            pltpu.SemaphoreType.DMA((g // 2,)),
+            pltpu.SemaphoreType.DMA((g,)),
+            pltpu.SemaphoreType.DMA((max(n_layer // 2 - 1, 1),)),
+            pltpu.SemaphoreType.DMA((max(n_layer // 2 - 1, 1),)),
             pltpu.SemaphoreType.DMA((n_layer - 1,)),
-            pltpu.SemaphoreType.DMA((n_layer - 1,)),
-            pltpu.SemaphoreType.DMA((n_layer - 1,)),
-            pltpu.SemaphoreType.DMA((n_layer - 1,)),
+            pltpu.SemaphoreType.DMA((n_layer // 2,)),
         ] + _permute_scratch(g) * (levels + 3),
         compiler_params=_params(cid),
     )(local_forest, local_root, factors, pattern, inverses, root_inverse)

time: 169 us -> 151 us (0.89); the launches traced: 166 us -> 150 us
  Pallas kernels: 161 us -> 145 us
    pallas_call x1, Pallas kernels: 161 us -> 145 us  [solve_all(): pl.pallas_call(kernel, out_shape=(jax.ShapeDtypeStruct(local_forest.shape...]
where the time goes in v9:
time: 151 us; the launch traced here: 150 us
  Pallas kernels  145 us (96%)
  local copies, waits for them, and re-layouts  4.73 us (3%)
    pallas_call x1, Pallas kernels, solve_all(): pl.pallas_call(kernel, out_shape=(jax.ShapeDtypeStruct(local_forest.shape...  145 us
    unnamed x2, local copies, waits for them, and re-layouts  3.33 us

profile of v9, /device:TPU:6, one launch (start us, length us, event | category | flops | bytes accessed | tf_op | source)
XLA Modules:
  0.0 150.2 jit_solution(14028377602739596573)
XLA Ops:
  0.6 1.4 copy.8.pat_ref
  2.0 144.9 %shard_map.77 = (bf16[3,4,32,512]{3,2,1,0:T(8,128)(2,1)}, bf16[1,4,32,512]{3,2,1,0:T(8,128)(2,1)}) custom-call(bf16[3,4,32,512]{3,2,1,0:T(8,128)(2,1)} %bitcast.9, bf16[1,4,32,512]{3,2,1,0:T(8,128)(2,1)} %bitcast.12, bf16[6,4,4,128,128]{4,3,2,1,0:T(8,128)(2,1)} %bitcast.8, s32[6,4,4]{2,1,0:T(4,128)} %copy.8.pat_ref, f32[3,128,128]{2,1,0:T(8,128)} %bitcast.11, ...), custom_call_target="tpu_custom_call" | custom-call | tf_op jit(solution)/shard_map/pallas_call | solution.py:446
  146.9 1.8 %copy.11 = bf16[1,384,512]{2,1,0:T(8,128)(2,1)} copy(bf16[1,384,512]{2,1,0:T(8,128)(2,1)} %bitcast.10) | data formatting | bytes 786432
  148.7 1.6 %copy.12 = bf16[128,512]{1,0:T(8,128)(2,1)} copy(bf16[128,512]{1,0:T(8,128)(2,1)} %bitcast.13) | data formatting | bytes 262144

commit v10 on v9

--- a/solution.py
+++ b/solution.py
@@ -295,7 +295,7 @@
         p = lax.axis_index("prow")
         q = lax.axis_index("pcol")
         me = lax.axis_index("layer")
-        perm = [perm_sems[3 * i:3 * i + 3] for i in range(levels + 3)]
+        perm = [perm_sems[3 * i:3 * i + 3] for i in range(levels + 4)]
         loads = [pltpu.make_async_copy(src, dst, load_sems.at[i]) for i, (src, dst) in
                  enumerate(((inv_hbm, inv_ref), (w_hbm, w_ref), (rinv_hbm, rinv_ref)))]
         for load in loads:
@@ -306,14 +306,18 @@
             pl.semaphore_signal(barrier, 1, device_id={"layer": (me + d) % n_layer},
                                 device_id_type=MESH)
         pl.semaphore_wait(barrier, g * g - 1 + n_layer - 1)
-        forest_in = _permute_start(f_ref, placed, True, *perm[0])
+        first_in = _permute_start(f_ref.at[pl.ds(0, 1)], placed.at[pl.ds(0, 1)], True, *perm[0])
+        rest_in = _permute_start(f_ref.at[pl.ds(1, levels - 1)], placed.at[pl.ds(1, levels - 1)],
+                                 True, *perm[levels + 3])
         root_in = _permute_start(r_ref, placed_root, True, *perm[1])
         tot[...] = jnp.zeros(tot.shape, f32)
-        forest_in()
+        first_in()
         pending = []
         outs = []
         loads[0].wait()
         for t in range(levels):
+            if t == 1:
+                rest_in()
             rhs = placed[t].reshape(rows, cols).astype(f32)
             if t > 0:
                 for copy in pending:
@@ -483,7 +487,7 @@
             pltpu.SemaphoreType.DMA((max(n_layer // 2 - 1, 1),)),
             pltpu.SemaphoreType.DMA((n_layer - 1,)),
             pltpu.SemaphoreType.DMA((n_layer // 2,)),
-        ] + _permute_scratch(g) * (levels + 3),
+        ] + _permute_scratch(g) * (levels + 4),
         compiler_params=_params(cid),
     )(local_forest, local_root, factors, pattern, inverses, root_inverse)
 

time: 151 us -> 147 us (0.974); the launches traced: 150 us -> 145 us
  Pallas kernels: 145 us -> 139 us
    pallas_call x1, Pallas kernels: 145 us -> 139 us  [solve_all(): pl.pallas_call(kernel, out_shape=(jax.ShapeDtypeStruct(local_forest.shape...]
where the time goes in v10:
time: 147 us; the launch traced here: 145 us
  Pallas kernels  139 us (95%)
  local copies, waits for them, and re-layouts  4.73 us (3%)
    pallas_call x1, Pallas kernels, solve_all(): pl.pallas_call(kernel, out_shape=(jax.ShapeDtypeStruct(local_forest.shape...  139 us
    unnamed x2, local copies, waits for them, and re-layouts  3.33 us

profile of v10, /device:TPU:6, one launch (start us, length us, event | category | flops | bytes accessed | tf_op | source)
XLA Modules:
  0.0 144.7 jit_solution(688472852094148149)
XLA Ops:
  0.6 1.4 copy.8.pat_ref
  2.0 139.3 %shard_map.77 = (bf16[3,4,32,512]{3,2,1,0:T(8,128)(2,1)}, bf16[1,4,32,512]{3,2,1,0:T(8,128)(2,1)}) custom-call(bf16[3,4,32,512]{3,2,1,0:T(8,128)(2,1)} %bitcast.9, bf16[1,4,32,512]{3,2,1,0:T(8,128)(2,1)} %bitcast.12, bf16[6,4,4,128,128]{4,3,2,1,0:T(8,128)(2,1)} %bitcast.8, s32[6,4,4]{2,1,0:T(4,128)} %copy.8.pat_ref, f32[3,128,128]{2,1,0:T(8,128)} %bitcast.11, ...), custom_call_target="tpu_custom_call" | custom-call | tf_op jit(solution)/shard_map/pallas_call | solution.py:450
  141.3 1.8 %copy.11 = bf16[1,384,512]{2,1,0:T(8,128)(2,1)} copy(bf16[1,384,512]{2,1,0:T(8,128)(2,1)} %bitcast.10) | data formatting | bytes 786432
  143.1 1.6 %copy.12 = bf16[128,512]{1,0:T(8,128)(2,1)} copy(bf16[128,512]{1,0:T(8,128)(2,1)} %bitcast.13) | data formatting | bytes 262144

commit v11 on v10

--- a/solution.py
+++ b/solution.py
@@ -309,7 +309,6 @@
         first_in = _permute_start(f_ref.at[pl.ds(0, 1)], placed.at[pl.ds(0, 1)], True, *perm[0])
         rest_in = _permute_start(f_ref.at[pl.ds(1, levels - 1)], placed.at[pl.ds(1, levels - 1)],
                                  True, *perm[levels + 3])
-        root_in = _permute_start(r_ref, placed_root, True, *perm[1])
         tot[...] = jnp.zeros(tot.shape, f32)
         first_in()
         pending = []
@@ -356,6 +355,8 @@
                     return carry
 
                 lax.fori_loop(0, g, body, 0)
+            if t == 0:
+                root_in = _permute_start(r_ref, placed_root, True, *perm[1])
             if t + 1 < levels:
                 pending = []
                 sb[t] = tot[t].astype(bf16)

time: 147 us -> 146 us (level)
  no operation moved by 1% of the time
where the time goes in v11:
time: 146 us; the launch traced here: 144 us
  Pallas kernels  138 us (95%)
  local copies, waits for them, and re-layouts  4.73 us (3%)
    pallas_call x1, Pallas kernels, solve_all(): pl.pallas_call(kernel, out_shape=(jax.ShapeDtypeStruct(local_forest.shape...  138 us
    unnamed x2, local copies, waits for them, and re-layouts  3.33 us

profile of v11, /device:TPU:6, one launch (start us, length us, event | category | flops | bytes accessed | tf_op | source)
XLA Modules:
  0.0 143.7 jit_solution(4725902035339724077)
XLA Ops:
  0.6 1.4 copy.8.pat_ref
  2.0 138.3 %shard_map.77 = (bf16[3,4,32,512]{3,2,1,0:T(8,128)(2,1)}, bf16[1,4,32,512]{3,2,1,0:T(8,128)(2,1)}) custom-call(bf16[3,4,32,512]{3,2,1,0:T(8,128)(2,1)} %bitcast.9, bf16[1,4,32,512]{3,2,1,0:T(8,128)(2,1)} %bitcast.12, bf16[6,4,4,128,128]{4,3,2,1,0:T(8,128)(2,1)} %bitcast.8, s32[6,4,4]{2,1,0:T(4,128)} %copy.8.pat_ref, f32[3,128,128]{2,1,0:T(8,128)} %bitcast.11, ...), custom_call_target="tpu_custom_call" | custom-call | tf_op jit(solution)/shard_map/pallas_call | solution.py:451
  140.4 1.8 %copy.11 = bf16[1,384,512]{2,1,0:T(8,128)(2,1)} copy(bf16[1,384,512]{2,1,0:T(8,128)(2,1)} %bitcast.10) | data formatting | bytes 786432
  142.1 1.6 %copy.12 = bf16[128,512]{1,0:T(8,128)(2,1)} copy(bf16[128,512]{1,0:T(8,128)(2,1)} %bitcast.13) | data formatting | bytes 262144

commit v12 on v11

--- a/solution.py
+++ b/solution.py
@@ -336,8 +336,6 @@
                     device_id={"prow": (p + d) % g}, device_id_type=MESH)
                 copy.start()
                 copies.append(copy)
-            outs.append(_permute_start(sol.at[pl.ds(t, 1)], fo_ref.at[pl.ds(t, 1)], False,
-                                       *perm[3 + t]))
             for copy in copies:
                 copy.wait()
             if t == 0:
@@ -373,6 +371,9 @@
             tot.at[levels - 1, pl.ds((1 - core) * half, half)], recv_a, a_sem.at[0], a_sem.at[1],
             device_id={"layer": me + 1 - 2 * core}, device_id_type=MESH)
         copy.start()
+        for t in range(levels):
+            outs.append(_permute_start(sol.at[pl.ds(t, 1)], fo_ref.at[pl.ds(t, 1)], False,
+                                       *perm[3 + t]))
         copy.wait()
         sbuf[...] = tot[levels - 1, pl.ds(core * half, half)] + recv_a[...]
         holder = q // half == core

time: 146 us -> 150 us (1.027); the launches traced: 144 us -> 150 us
  Pallas kernels: 138 us -> 145 us
    pallas_call x1, Pallas kernels: 138 us -> 145 us  [solve_all(): pl.pallas_call(kernel, out_shape=(jax.ShapeDtypeStruct(local_forest.shape...]
where the time goes in v12:
time: 150 us
  Pallas kernels  145 us (97%)
  local copies, waits for them, and re-layouts  4.73 us (3%)
    pallas_call x1, Pallas kernels, solve_all(): pl.pallas_call(kernel, out_shape=(jax.ShapeDtypeStruct(local_forest.shape...  145 us
    unnamed x2, local copies, waits for them, and re-layouts  3.33 us

profile of v12, /device:TPU:6, one launch (start us, length us, event | category | flops | bytes accessed | tf_op | source)
XLA Modules:
  0.0 149.9 jit_solution(9370069960480263162)
XLA Ops:
  0.6 1.4 copy.8.pat_ref
  2.0 144.5 %shard_map.77 = (bf16[3,4,32,512]{3,2,1,0:T(8,128)(2,1)}, bf16[1,4,32,512]{3,2,1,0:T(8,128)(2,1)}) custom-call(bf16[3,4,32,512]{3,2,1,0:T(8,128)(2,1)} %bitcast.9, bf16[1,4,32,512]{3,2,1,0:T(8,128)(2,1)} %bitcast.12, bf16[6,4,4,128,128]{4,3,2,1,0:T(8,128)(2,1)} %bitcast.8, s32[6,4,4]{2,1,0:T(4,128)} %copy.8.pat_ref, f32[3,128,128]{2,1,0:T(8,128)} %bitcast.11, ...), custom_call_target="tpu_custom_call" | custom-call | tf_op jit(solution)/shard_map/pallas_call | solution.py:452
  146.6 1.8 %copy.11 = bf16[1,384,512]{2,1,0:T(8,128)(2,1)} copy(bf16[1,384,512]{2,1,0:T(8,128)(2,1)} %bitcast.10) | data formatting | bytes 786432
  148.3 1.6 %copy.12 = bf16[128,512]{1,0:T(8,128)(2,1)} copy(bf16[128,512]{1,0:T(8,128)(2,1)} %bitcast.13) | data formatting | bytes 262144

commit v13 on v11

--- a/solution.py
+++ b/solution.py
@@ -418,25 +418,28 @@
             part[...] = total
             full[mine] = total
             copies = []
-            for d in range(1, n_layer):
+            for dm in range(1, n_h):
+                pm = (m + dm) % n_h
                 copy = pltpu.make_async_remote_copy(
-                    part, full.at[mine], hs.at[d - 1], hr.at[m],
-                    device_id={"layer": (me + d) % n_layer}, device_id_type=MESH)
+                    part, full.at[mine], hs.at[dm - 1], hr.at[m],
+                    device_id={"layer": 2 * pm + core}, device_id_type=MESH)
                 copy.start()
                 copies.append(copy)
             for copy in copies:
                 copy.wait_send()
-
-        for dm in range(n_h):
-            mm = (m + dm) % n_h
-            arrival = pltpu.make_async_copy(
-                part, full.at[pl.ds(pl.multiple_of(mm * c_rows, 8), c_rows)], hr.at[mm])
-            if dm == 0:
-                @pl.when(jnp.logical_not(holder))
-                def _():
-                    arrival.wait()
-            else:
-                arrival.wait()
+            for dm in range(1, n_h):
+                mm = (m + dm) % n_h
+                pltpu.make_async_copy(
+                    part, full.at[pl.ds(pl.multiple_of(mm * c_rows, 8), c_rows)], hr.at[mm]).wait()
+            copy = pltpu.make_async_remote_copy(
+                full, full, hs.at[n_layer - 2], hr.at[n_h],
+                device_id={"layer": me + 1 - 2 * core}, device_id_type=MESH)
+            copy.start()
+            copy.wait_send()
+
+        @pl.when(jnp.logical_not(holder))
+        def _():
+            pltpu.make_async_copy(full, full, hr.at[n_h]).wait()
         root_in()
         loads[2].wait()
         side = placed_root[0].reshape(rows, cols).astype(f32) - full[...]
@@ -487,7 +490,7 @@
             pltpu.SemaphoreType.DMA((max(n_layer // 2 - 1, 1),)),
             pltpu.SemaphoreType.DMA((max(n_layer // 2 - 1, 1),)),
             pltpu.SemaphoreType.DMA((n_layer - 1,)),
-            pltpu.SemaphoreType.DMA((n_layer // 2,)),
+            pltpu.SemaphoreType.DMA((n_layer // 2 + 1,)),
         ] + _permute_scratch(g) * (levels + 4),
         compiler_params=_params(cid),
     )(local_forest, local_root, factors, pattern, inverses, root_inverse)

time: 146 us -> 145 us (level)
  the two profiles are of different devices: /device:TPU:6 before, /device:TPU:58 now
where the time goes in v13:
time: 145 us; the launch traced here: 144 us
  Pallas kernels  139 us (96%)
  local copies, waits for them, and re-layouts  4.73 us (3%)
    pallas_call x1, Pallas kernels, solve_all(): pl.pallas_call(kernel, out_shape=(jax.ShapeDtypeStruct(local_forest.shape...  139 us
    unnamed x2, local copies, waits for them, and re-layouts  3.33 us

profile of v13, /device:TPU:58, one launch (start us, length us, event | category | flops | bytes accessed | tf_op | source)
XLA Modules:
  0.0 144.5 jit_solution(14106775972635441116)
XLA Ops:
  0.6 1.4 copy.8.pat_ref
  2.0 139.1 %shard_map.77 = (bf16[3,4,32,512]{3,2,1,0:T(8,128)(2,1)}, bf16[1,4,32,512]{3,2,1,0:T(8,128)(2,1)}) custom-call(bf16[3,4,32,512]{3,2,1,0:T(8,128)(2,1)} %bitcast.9, bf16[1,4,32,512]{3,2,1,0:T(8,128)(2,1)} %bitcast.12, bf16[6,4,4,128,128]{4,3,2,1,0:T(8,128)(2,1)} %bitcast.8, s32[6,4,4]{2,1,0:T(4,128)} %copy.8.pat_ref, f32[3,128,128]{2,1,0:T(8,128)} %bitcast.11, ...), custom_call_target="tpu_custom_call" | custom-call | tf_op jit(solution)/shard_map/pallas_call | solution.py:454
  141.2 1.8 %copy.11 = bf16[1,384,512]{2,1,0:T(8,128)(2,1)} copy(bf16[1,384,512]{2,1,0:T(8,128)(2,1)} %bitcast.10) | data formatting | bytes 786432
  142.9 1.6 %copy.12 = bf16[128,512]{1,0:T(8,128)(2,1)} copy(bf16[128,512]{1,0:T(8,128)(2,1)} %bitcast.13) | data formatting | bytes 262144

commit v14 on v13

--- a/solution.py
+++ b/solution.py
@@ -355,18 +355,18 @@
                     return carry
 
                 lax.fori_loop(0, g, body, 0)
-            if t == 0:
-                root_in = _permute_start(r_ref, placed_root, True, *perm[1])
-            if t + 1 < levels:
-                pending = []
-                sb[t] = tot[t].astype(bf16)
-                for d in range(1, g):
-                    peer = (q + d) % g
-                    copy = pltpu.make_async_remote_copy(
-                        sb.at[t, peer], rrecv.at[t, d - 1], rs_s.at[t, d - 1], rs_r.at[t, d - 1],
-                        device_id={"pcol": peer}, device_id_type=MESH)
-                    copy.start()
-                    pending.append(copy)
+                if target == t + 1 and target < levels:
+                    pending = []
+                    sb[t] = tot[t].astype(bf16)
+                    for d in range(1, g):
+                        peer = (q + d) % g
+                        copy = pltpu.make_async_remote_copy(
+                            sb.at[t, peer], rrecv.at[t, d - 1], rs_s.at[t, d - 1],
+                            rs_r.at[t, d - 1], device_id={"pcol": peer}, device_id_type=MESH)
+                        copy.start()
+                        pending.append(copy)
+                if t == 0 and target == t + 1:
+                    root_in = _permute_start(r_ref, placed_root, True, *perm[1])
         core = me % 2
         half = g // 2
         copy = pltpu.make_async_remote_copy(

time: 145 us -> 140 us (0.966)
  the two profiles are of different devices: /device:TPU:58 before, /device:TPU:2 now
where the time goes in v14:
time: 140 us
  Pallas kernels  134 us (96%)
  local copies, waits for them, and re-layouts  4.73 us (3%)
    pallas_call x1, Pallas kernels, solve_all(): pl.pallas_call(kernel, out_shape=(jax.ShapeDtypeStruct(local_forest.shape...  134 us
    unnamed x2, local copies, waits for them, and re-layouts  3.33 us

profile of v14, /device:TPU:2, one launch (start us, length us, event | category | flops | bytes accessed | tf_op | source)
XLA Modules:
  0.0 139.8 jit_solution(3768114215490895473)
XLA Ops:
  0.6 1.4 copy.8.pat_ref
  2.0 134.5 %shard_map.77 = (bf16[3,4,32,512]{3,2,1,0:T(8,128)(2,1)}, bf16[1,4,32,512]{3,2,1,0:T(8,128)(2,1)}) custom-call(bf16[3,4,32,512]{3,2,1,0:T(8,128)(2,1)} %bitcast.9, bf16[1,4,32,512]{3,2,1,0:T(8,128)(2,1)} %bitcast.12, bf16[6,4,4,128,128]{4,3,2,1,0:T(8,128)(2,1)} %bitcast.8, s32[6,4,4]{2,1,0:T(4,128)} %copy.8.pat_ref, f32[3,128,128]{2,1,0:T(8,128)} %bitcast.11, ...), custom_call_target="tpu_custom_call" | custom-call | tf_op jit(solution)/shard_map/pallas_call | solution.py:454
  136.5 1.8 %copy.11 = bf16[1,384,512]{2,1,0:T(8,128)(2,1)} copy(bf16[1,384,512]{2,1,0:T(8,128)(2,1)} %bitcast.10) | data formatting | bytes 786432
  138.3 1.6 %copy.12 = bf16[128,512]{1,0:T(8,128)(2,1)} copy(bf16[128,512]{1,0:T(8,128)(2,1)} %bitcast.13) | data formatting | bytes 262144

commit v15 on v14

--- a/solution.py
+++ b/solution.py
@@ -369,14 +369,19 @@
                     root_in = _permute_start(r_ref, placed_root, True, *perm[1])
         core = me % 2
         half = g // 2
-        copy = pltpu.make_async_remote_copy(
-            tot.at[levels - 1, pl.ds((1 - core) * half, half)], recv_a, a_sem.at[0], a_sem.at[1],
-            device_id={"layer": me + 1 - 2 * core}, device_id_type=MESH)
-        copy.start()
-        copy.wait()
-        sbuf[...] = tot[levels - 1, pl.ds(core * half, half)] + recv_a[...]
+        exchanges = []
+        for k in range(half):
+            copy = pltpu.make_async_remote_copy(
+                tot.at[levels - 1, (1 - core) * half + k], recv_a.at[k],
+                a_sem.at[2 * k], a_sem.at[2 * k + 1],
+                device_id={"layer": me + 1 - 2 * core}, device_id_type=MESH)
+            copy.start()
+            exchanges.append(copy)
         holder = q // half == core
+        sends = []
         for k in range(half):
+            exchanges[k].wait()
+            sbuf[k] = tot[levels - 1, core * half + k] + recv_a[k]
             j = core * half + k
             off = (j - q + g) % g
             copy = pltpu.make_async_remote_copy(
@@ -386,6 +391,11 @@
             @pl.when(j != q)
             def _(copy=copy):
                 copy.start()
+
+            sends.append((copy, j))
+        for copy, j in sends:
+            @pl.when(j != q)
+            def _(copy=copy):
                 copy.wait_send()
 
         n_h = n_layer // 2
@@ -484,7 +494,7 @@
             pltpu.SemaphoreType.DMA((levels, g - 1)),
             pltpu.SemaphoreType.DMA((levels, g - 1)),
             pltpu.SemaphoreType.DMA((levels, g - 1)),
-            pltpu.SemaphoreType.DMA((2,)),
+            pltpu.SemaphoreType.DMA((g,)),
             pltpu.SemaphoreType.DMA((g // 2,)),
             pltpu.SemaphoreType.DMA((g,)),
             pltpu.SemaphoreType.DMA((max(n_layer // 2 - 1, 1),)),

time: 140 us -> 137 us (0.979)
  the two profiles are of different devices: /device:TPU:2 before, /device:TPU:6 now
where the time goes in v15:
time: 137 us; the launch traced here: 135 us
  Pallas kernels  130 us (95%)
  local copies, waits for them, and re-layouts  4.73 us (3%)
    pallas_call x1, Pallas kernels, solve_all(): pl.pallas_call(kernel, out_shape=(jax.ShapeDtypeStruct(local_forest.shape...  130 us
    unnamed x2, local copies, waits for them, and re-layouts  3.33 us

profile of v15, /device:TPU:6, one launch (start us, length us, event | category | flops | bytes accessed | tf_op | source)
XLA Modules:
  0.0 135.4 jit_solution(18156010004748923874)
XLA Ops:
  0.6 1.4 %copy.8.pat_ref = s32[6,4,4]{2,1,0:T(4,128)} copy(s32[6,4,4]{0,2,1:T(4,128)} %bitcast.15) | data formatting | bytes 768 | tf_op jit(solution)/shard_map/reshape | solution.py:518
  2.0 130.0 %shard_map.77 = (bf16[3,4,32,512]{3,2,1,0:T(8,128)(2,1)}, bf16[1,4,32,512]{3,2,1,0:T(8,128)(2,1)}) custom-call(bf16[3,4,32,512]{3,2,1,0:T(8,128)(2,1)} %bitcast.9, bf16[1,4,32,512]{3,2,1,0:T(8,128)(2,1)} %bitcast.12, bf16[6,4,4,128,128]{4,3,2,1,0:T(8,128)(2,1)} %bitcast.8, s32[6,4,4]{2,1,0:T(4,128)} %copy.8.pat_ref, f32[3,128,128]{2,1,0:T(8,128)} %bitcast.11, ...), custom_call_target="tpu_custom_call" | custom-call | tf_op jit(solution)/shard_map/pallas_call | solution.py:464
  132.1 1.8 %copy.11 = bf16[1,384,512]{2,1,0:T(8,128)(2,1)} copy(bf16[1,384,512]{2,1,0:T(8,128)(2,1)} %bitcast.10) | data formatting | bytes 786432
  133.8 1.6 %copy.12 = bf16[128,512]{1,0:T(8,128)(2,1)} copy(bf16[128,512]{1,0:T(8,128)(2,1)} %bitcast.13) | data formatting | bytes 262144

commit v16 on v15

--- a/solution.py
+++ b/solution.py
@@ -357,9 +357,9 @@
                 lax.fori_loop(0, g, body, 0)
                 if target == t + 1 and target < levels:
                     pending = []
-                    sb[t] = tot[t].astype(bf16)
                     for d in range(1, g):
                         peer = (q + d) % g
+                        sb[t, peer] = tot[t, peer].astype(bf16)
                         copy = pltpu.make_async_remote_copy(
                             sb.at[t, peer], rrecv.at[t, d - 1], rs_s.at[t, d - 1],
                             rs_r.at[t, d - 1], device_id={"pcol": peer}, device_id_type=MESH)

time: 137 us -> 137 us (level)
  no operation moved by 1% of the time
where the time goes in v16:
time: 137 us
  Pallas kernels  131 us (96%)
  local copies, waits for them, and re-layouts  4.73 us (3%)
    pallas_call x1, Pallas kernels, solve_all(): pl.pallas_call(kernel, out_shape=(jax.ShapeDtypeStruct(local_forest.shape...  131 us
    unnamed x2, local copies, waits for them, and re-layouts  3.33 us

profile of v16, /device:TPU:6, one launch (start us, length us, event | category | flops | bytes accessed | tf_op | source)
XLA Modules:
  0.0 136.6 jit_solution(756803688409403421)
XLA Ops:
  0.6 1.4 %copy.8.pat_ref = s32[6,4,4]{2,1,0:T(4,128)} copy(s32[6,4,4]{0,2,1:T(4,128)} %bitcast.15) | data formatting | bytes 768 | tf_op jit(solution)/shard_map/reshape | solution.py:518
  2.0 131.3 %shard_map.77 = (bf16[3,4,32,512]{3,2,1,0:T(8,128)(2,1)}, bf16[1,4,32,512]{3,2,1,0:T(8,128)(2,1)}) custom-call(bf16[3,4,32,512]{3,2,1,0:T(8,128)(2,1)} %bitcast.9, bf16[1,4,32,512]{3,2,1,0:T(8,128)(2,1)} %bitcast.12, bf16[6,4,4,128,128]{4,3,2,1,0:T(8,128)(2,1)} %bitcast.8, s32[6,4,4]{2,1,0:T(4,128)} %copy.8.pat_ref, f32[3,128,128]{2,1,0:T(8,128)} %bitcast.11, ...), custom_call_target="tpu_custom_call" | custom-call | tf_op jit(solution)/shard_map/pallas_call | solution.py:464
  133.3 1.8 %copy.11 = bf16[1,384,512]{2,1,0:T(8,128)(2,1)} copy(bf16[1,384,512]{2,1,0:T(8,128)(2,1)} %bitcast.10) | data formatting | bytes 786432
  135.1 1.6 %copy.12 = bf16[128,512]{1,0:T(8,128)(2,1)} copy(bf16[128,512]{1,0:T(8,128)(2,1)} %bitcast.13) | data formatting | bytes 262144
